TPU v7x, 256 devices: a whole 4x4x8 slice. The times are simulated.
256 devices in a mesh: expert: 64 (over z, y, core), replica: 4 (over x).
Axes of the slice: x: 4, y: 4, z: 8, core: 2. Of those that a mesh axis runs over, the one named last changes fastest.
Arguments:
- hidden_first: bfloat16 [2048, 4096], P(('expert', 'replica')), may hold values from -40 to 40
- hidden_second: bfloat16 [2048, 4096], P(('expert', 'replica')), may hold values from -40 to 40
- routes_first: int32 [2048, 8], P(('expert', 'replica')), may hold values from 0 to 63, all different within a row; in each aligned block of 8 rows (0 to 7, 8 to 15, ...) at most 2 rows name the same one
- routes_second: int32 [2048, 8], P(('expert', 'replica')), may hold values from 0 to 63, all different within a row; in each aligned block of 8 rows (0 to 7, 8 to 15, ...) at most 2 rows name the same one
- mixing_first: float32 [2048, 8], P(('expert', 'replica')), may hold values from 0.05 to 0.5
- mixing_second: float32 [2048, 8], P(('expert', 'replica')), may hold values from 0.05 to 0.5
- norm_gain: float32 [4096], replicated, may hold values from 0.1 to 1.9
- expert_owner: int32 [64], replicated, may hold values from 0 to 63, each once
- swap_flags: int32 [64], replicated, may hold values from 0 to 1, as said below
- gate_up_values: bfloat16 [64, 2, 4096, 1024], P('expert', None, None, 'replica'), may hold values from -0.09375 to 0.09375
- gate_up_scales: bfloat16 [64, 2, 32, 8], P('expert', None, None, 'replica'), may hold values from 0.5 to 2
- down_values: bfloat16 [64, 1024, 4096], P('expert', 'replica'), may hold values from -0.1875 to 0.1875
- down_scales: bfloat16 [64, 8, 32], P('expert', 'replica'), may hold values from 0.5 to 2
Outputs:
- output_first: bfloat16 [2048, 4096], P(('expert', 'replica'))
- output_second: bfloat16 [2048, 4096], P(('expert', 'replica'))
- gate_up_moved: bfloat16 [64, 2, 4096, 1024], P('expert', None, None, 'replica')
- gate_up_scales_moved: bfloat16 [64, 2, 32, 8], P('expert', None, None, 'replica')
- down_moved: bfloat16 [64, 1024, 4096], P('expert', 'replica')
- down_scales_moved: bfloat16 [64, 8, 32], P('expert', 'replica')
Inputs may be any that keep to these rules, and one draw needn't show every extreme that they name: swap_flags[d] equals swap_flags[(d + 32) mod 64].
All inputs are finite; a program needn't handle non-finite values.
Results may differ from a plain program's by a relative error of at most 0.012.
Values may be sent and summed in bfloat16 or wider, within the bound.
No kernel may reach another device: no remote copies, remote signals or barrier semaphores. Data moves between devices by JAX's collectives and lax.ppermute only.
A program may use at most 128 MiB of HBM per device.

v0:
```python
import jax
import jax.numpy as jnp
from jax import lax
from jax.sharding import PartitionSpec as P


def partner(block, axis, bit):
    count = lax.axis_size(axis)
    route = []
    for low in range(count):
        high = low | 1 << bit
        if high != low and high < count:
            route += [(low, high), (high, low)]
    return lax.ppermute(block, axis, route)


def dequantize(values, scales):
    height, breadth = (values.shape[-2], values.shape[-1])
    block_rows, block_cols = (scales.shape[-2], scales.shape[-1])
    leading = values.shape[:-2]
    blocked = values.astype(jnp.float32).reshape(
        leading + (block_rows, height // block_rows, block_cols, breadth // block_cols)
    )
    scaled = blocked * scales.astype(jnp.float32)[..., :, None, :, None]
    return scaled.reshape(values.shape).astype(jnp.bfloat16)


def rms_normed(hidden, norm_gain):
    widened = hidden.astype(jnp.float32)
    inverse_rms = lax.rsqrt(jnp.mean(widened * widened, axis=-1, keepdims=True) + 1e-06)
    return (widened * inverse_rms * norm_gain).astype(jnp.bfloat16)


def rounded(partial_sum):
    return lax.optimization_barrier(partial_sum.astype(jnp.bfloat16)).astype(jnp.float32)


def expert_partial(token_rows, weights):
    gate_up, down_proj = weights
    gate_act = jnp.dot(token_rows, gate_up[0], preferred_element_type=jnp.float32)
    up_act = jnp.dot(token_rows, gate_up[1], preferred_element_type=jnp.float32)
    inner_act = (jax.nn.silu(gate_act) * up_act).astype(jnp.bfloat16)
    return rounded(jnp.dot(inner_act, down_proj, preferred_element_type=jnp.float32))


def pick_slots(routes, owner_slots, experts, capacity):
    tokens_here, top_count = routes.shape
    expert_ids = jnp.arange(owner_slots.shape[0], dtype=jnp.int32)
    target = jnp.sum(jnp.where(routes[:, :, None] == expert_ids, owner_slots, 0), axis=-1).reshape(
        -1
    )
    device_ids = jnp.arange(experts, dtype=jnp.int32)
    target_hot = (target[:, None] == device_ids).astype(jnp.int32)
    earlier = jnp.cumsum(target_hot, axis=0) - target_hot
    rank_in = jnp.sum(earlier * target_hot, axis=1)
    slot_ids = target * capacity + rank_in
    columns = jnp.arange(experts * capacity, dtype=jnp.int32)
    return (
        (slot_ids[:, None] == columns)
        .astype(jnp.float32)
        .reshape(tokens_here, top_count, experts * capacity)
    )


def finish(partial_terms):
    summed = lax.psum_scatter(
        partial_terms.astype(jnp.bfloat16), "replica", scatter_dimension=0, tiled=True
    )
    return lax.all_to_all(summed, "expert", split_axis=1, concat_axis=1, tiled=True)


def decode_step(hidden, routes, mixing, norm_gain, owner_slots, weights):
    experts = lax.axis_size("expert")
    copies = lax.axis_size("replica")
    tokens_here, top_count = routes.shape
    features = hidden.shape[1]
    capacity = min(tokens_here, max(2, 2 * tokens_here * top_count // experts))
    normed = rms_normed(hidden, norm_gain)
    own_picks = pick_slots(routes, owner_slots, experts, capacity)
    pooled, pooled_routes = (
        lax.all_gather(normed, "replica", axis=0, tiled=True),
        lax.all_gather(routes, "replica", axis=0, tiled=True),
    )
    grouped = pooled_routes.reshape(copies, tokens_here, top_count)
    pick_table = jax.vmap(
        lambda route_group: pick_slots(route_group, owner_slots, experts, capacity)
    )(grouped)
    placing = jnp.sum(pick_table, axis=2).astype(jnp.bfloat16)
    outgoing = jnp.einsum(
        "rts,rtd->rsd",
        placing,
        pooled.reshape(copies, tokens_here, features),
        preferred_element_type=jnp.float32,
    )
    outgoing = outgoing.astype(jnp.bfloat16).reshape(copies, experts, capacity, features)
    arrived = lax.all_to_all(outgoing, "expert", split_axis=1, concat_axis=1, tiled=True)
    slot_count = arrived.shape[2]
    flat_rows = arrived.reshape(-1, features)
    partial_terms = expert_partial(flat_rows, weights).reshape(
        copies, experts, slot_count, features
    )
    returned = finish(partial_terms)
    mixing_matrix = jnp.einsum("tks,tk->ts", own_picks, mixing, precision=lax.Precision.HIGHEST)
    merged = jnp.dot(
        mixing_matrix,
        returned.reshape(experts * capacity, features).astype(jnp.float32),
        precision=lax.Precision.HIGHEST,
    )
    return merged.astype(jnp.bfloat16)


def body(
    hidden_first,
    hidden_second,
    routes_first,
    routes_second,
    mixing_first,
    mixing_second,
    norm_gain,
    expert_owner,
    swap_flags,
    gate_up_values,
    gate_up_scales,
    down_values,
    down_scales,
):
    experts = lax.axis_size("expert")
    halfway = experts // 2
    my_slot = lax.axis_index("expert")
    current = (gate_up_values, gate_up_scales, down_values, down_scales)
    incoming = partner(
        (gate_up_values, gate_up_scales, down_values, down_scales),
        "expert",
        experts.bit_length() - 2,
    )
    slot_ids = jnp.arange(experts, dtype=jnp.int32)
    flagged = jnp.sum(jnp.where(slot_ids == my_slot, swap_flags, 0)) == 1
    moved_arrays = tuple(
        (
            jnp.where(flagged, fresh_piece, stale_piece)
            for fresh_piece, stale_piece in zip(incoming, current)
        )
    )
    weights_before = (
        dequantize(gate_up_values[0], gate_up_scales[0]),
        dequantize(down_values[0], down_scales[0]),
    )
    output_first = decode_step(
        hidden_first, routes_first, mixing_first, norm_gain, expert_owner, weights_before
    )
    owner_flags = jnp.sum(jnp.where(expert_owner[:, None] == slot_ids, swap_flags, 0), axis=1)
    owner_after = jnp.where(owner_flags == 1, (expert_owner + halfway) % experts, expert_owner)
    weights_after = (
        dequantize(moved_arrays[0][0], moved_arrays[1][0]),
        dequantize(moved_arrays[2][0], moved_arrays[3][0]),
    )
    output_second = decode_step(
        hidden_second, routes_second, mixing_second, norm_gain, owner_after, weights_after
    )
    return (
        output_first,
        output_second,
        moved_arrays[0],
        moved_arrays[1],
        moved_arrays[2],
        moved_arrays[3],
    )


def solution(mesh):
    return jax.shard_map(
        body,
        mesh=mesh,
        in_specs=(
            P(("expert", "replica"), None),
            P(("expert", "replica"), None),
            P(("expert", "replica"), None),
            P(("expert", "replica"), None),
            P(("expert", "replica"), None),
            P(("expert", "replica"), None),
            P(),
            P(),
            P(),
            P("expert", None, None, "replica"),
            P("expert", None, None, "replica"),
            P("expert", "replica", None),
            P("expert", "replica", None),
        ),
        out_specs=(
            P(("expert", "replica"), None),
            P(("expert", "replica"), None),
            P("expert", None, None, "replica"),
            P("expert", None, None, "replica"),
            P("expert", "replica", None),
            P("expert", "replica", None),
        ),
        check_vma=False,
    )
```

profile of v0, /device:TPU:1, one launch (start us, length us, event | category | flops | bytes accessed | tf_op | source)
XLA Modules:
  0.0 738.2 jit_solution(4624766096503249148)
XLA Ops:
  8.7 10.4 %all_gather.14 = s32[32,8]{1,0:T(8,128)S(1)} all-gather(s32[8,8]{1,0:T(8,128)} %param.16), channel_id=1, replica_groups=mesh['expert'=64,'replica'=4] {'replica'}, dimensions={0}, use_global_device_ids=true | all-gather | bytes 1280 | tf_op jit(solution)/shard_map/all_gather | solution.py:82
  23.6 9.4 %all_gather.15 = bf16[32,4096]{1,0:T(8,128)(2,1)S(1)} all-gather(bf16[8,4096]{1,0:T(8,128)(2,1)S(1)} %get-tuple-element.13), channel_id=1, replica_groups=mesh['expert'=64,'replica'=4] {'replica'}, dimensions={0}, use_global_device_ids=true | all-gather | bytes 327680 | tf_op jit(solution)/shard_map/all_gather | solution.py:81
  36.3 7.6 %reshape.189 = bf16[4,64,2,4096]{3,2,1,0:T(2,128)(2,1)} reshape(bf16[4,128,4096]{2,1,0:T(8,128)(2,1)} %convolution_convert_fusion.1) | data formatting | bytes 8388608 | tf_op jit(solution)/shard_map/reshape | solution.py:95
  43.9 10.2 %copy.44 = bf16[4,64,2,4096]{3,2,0,1:T(2,128)(2,1)} copy(bf16[4,64,2,4096]{3,2,1,0:T(2,128)(2,1)} %reshape.189) | data formatting | bytes 8388608 | tf_op jit(solution)/shard_map/reshape | solution.py:95
  54.1 18.4 %all-to-all-start.2 = ((bf16[4,64,2,4096]{3,2,0,1:T(2,128)(2,1)}), bf16[4,64,2,4096]{3,2,0,1:T(2,128)(2,1)}, u32[]{:S(2)}, u32[]{:S(2)}) async-start(bf16[4,64,2,4096]{3,2,0,1:T(2,128)(2,1)} %copy.44), calls=%async_computation.3 | async-start | bytes 8388608 | tf_op jit(solution)/shard_map/all_to_all | solution.py:96
  83.5 10.1 %all_gather.12 = s32[32,8]{1,0:T(8,128)S(1)} all-gather(s32[8,8]{1,0:T(8,128)S(1)} %copy-done.4), channel_id=1, replica_groups=mesh['expert'=64,'replica'=4] {'replica'}, dimensions={0}, use_global_device_ids=true | all-gather | bytes 1280 | tf_op jit(solution)/shard_map/all_gather | solution.py:82
  94.9 10.6 %all_gather.13 = bf16[32,4096]{1,0:T(8,128)(2,1)S(1)} all-gather(bf16[8,4096]{1,0:T(8,128)(2,1)S(1)} %get-tuple-element.14), channel_id=1, replica_groups=mesh['expert'=64,'replica'=4] {'replica'}, dimensions={0}, use_global_device_ids=true | all-gather | bytes 327680 | tf_op jit(solution)/shard_map/all_gather | solution.py:81
  108.9 7.8 %reshape.185 = bf16[4,64,2,4096]{3,2,1,0:T(2,128)(2,1)} reshape(bf16[4,128,4096]{2,1,0:T(8,128)(2,1)} %convolution_convert_fusion.3) | data formatting | bytes 8388608 | tf_op jit(solution)/shard_map/reshape | solution.py:95
  116.8 10.2 %copy.39 = bf16[4,64,2,4096]{3,2,0,1:T(2,128)(2,1)} copy(bf16[4,64,2,4096]{3,2,1,0:T(2,128)(2,1)} %reshape.185) | data formatting | bytes 8388608 | tf_op jit(solution)/shard_map/reshape | solution.py:95
  128.2 243.6 %collective-permute-done.3 = bf16[1,2,32]{2,1,0:T(2,128)(2,1)S(1)} collective-permute-done((bf16[1,2,32]{2,1,0:T(2,128)(2,1)S(1)}, bf16[1,2,32]{2,1,0:T(2,128)(2,1)S(1)}, u32[]{:S(2)}, u32[]{:S(2)}) %collective-permute-start.3) | collective-permute-done | bytes 160 | tf_op jit(solution)/shard_map/ppermute | solution.py:14
  378.5 11.5 %mul.143 = f32[2,4096,256]{2,1,0:T(8,128)} reshape(f32[2,32,128,2,128]{4,3,2,1,0:T(2,128)} %mul.142) | data formatting | bytes 16777216 | tf_op jit(solution)/shard_map/mul | solution.py:24
  395.5 11.5 %mul.159 = f32[2,4096,256]{2,1,0:T(8,128)} reshape(f32[2,32,128,2,128]{4,3,2,1,0:T(2,128)} %mul.158) | data formatting | bytes 16777216 | tf_op jit(solution)/shard_map/mul | solution.py:24
  409.9 10.6 %fusion = (bf16[2,4096,256]{2,1,0:T(8,128)(2,1)}, bf16[1,2,4096,256]{3,2,1,0:T(8,128)(2,1)}, bf16[2,4096,256]{2,1,0:T(8,128)(2,1)}) fusion(f32[2,4096,256]{2,1,0:T(8,128)} %mul.159, bf16[1,2,4096,256]{3,2,1,0:T(8,128)(2,1)} %collective-permute-done, bf16[1,2,4096,256]{3,2,1,0:T(8,128)(2,1)S(1)} %copy-done.2, pred[]{:T(512)S(6)} %eq.251, f32[2,4096,256]{2,1,0:T(8,128)} %mul.143), kind=kLoop, calls=%fused_computation.1 | loop fusion | flops 14680064 | bytes 37748736 | tf_op jit(solution)/shard_map/convert_element_type | solution.py:25
  420.5 75.5 %all-to-all-start = ((bf16[4,64,2,4096]{3,2,0,1:T(2,128)(2,1)}), bf16[4,64,2,4096]{3,2,0,1:T(2,128)(2,1)}, u32[]{:S(2)}, u32[]{:S(2)}) async-start(bf16[4,64,2,4096]{3,2,0,1:T(2,128)(2,1)} %copy.39), calls=%async_computation | async-start | bytes 8388608 | tf_op jit(solution)/shard_map/all_to_all | solution.py:96
  496.0 9.7 %copy.45 = bf16[4,64,2,4096]{3,2,1,0:T(2,128)(2,1)} copy(bf16[4,64,2,4096]{3,2,0,1:T(2,128)(2,1)} %all-to-all-done.2) | data formatting | bytes 8388608 | tf_op jit(solution)/shard_map/all_to_all | solution.py:96
  519.8 11.9 %convolution_convert_fusion = bf16[512,4096]{1,0:T(8,128)(2,1)} fusion(f32[32,8,32,128]{3,2,1,0:T(8,128)} %bitcast.101, bf16[1,256,4096]{2,1,0:T(8,128)(2,1)} %broadcast_select_fusion.1, f32[512,256]{1,0:T(8,128)S(1)} %fusion.6, bf16[512,4096]{1,0:T(8,128)(2,1)} %reshape.190, bf16[2,4096,256]{2,1,0:T(8,128)(2,1)} %get-tuple-element.6), kind=kOutput, calls=%fused_computation.4 | convolution fusion | flops 2153512960 | bytes 17301504 | tf_op jit(solution)/shard_map/dot_general | solution.py:43
  531.7 7.6 %convert_element_type.200 = bf16[4,64,2,4096]{3,2,1,0:T(2,128)(2,1)} reshape(bf16[512,4096]{1,0:T(8,128)(2,1)} %convolution_convert_fusion) | data formatting | bytes 8388608 | tf_op jit(solution)/shard_map/convert_element_type | solution.py:67
  546.5 44.4 %all-to-all-done = bf16[4,64,2,4096]{3,2,0,1:T(2,128)(2,1)} async-done(((bf16[4,64,2,4096]{3,2,0,1:T(2,128)(2,1)}), bf16[4,64,2,4096]{3,2,0,1:T(2,128)(2,1)}, u32[]{:S(2)}, u32[]{:S(2)}) %all-to-all-start) | async-done | bytes 4194336 | tf_op jit(solution)/shard_map/all_to_all | solution.py:96
  590.9 9.7 %copy.40 = bf16[4,64,2,4096]{3,2,1,0:T(2,128)(2,1)} copy(bf16[4,64,2,4096]{3,2,0,1:T(2,128)(2,1)} %all-to-all-done) | data formatting | bytes 8388608 | tf_op jit(solution)/shard_map/all_to_all | solution.py:96
  614.7 11.4 %convolution_convert_fusion.2 = bf16[512,4096]{1,0:T(8,128)(2,1)} fusion(f32[32,8,32,128]{3,2,1,0:T(8,128)} %bitcast.102, bf16[1,256,4096]{2,1,0:T(8,128)(2,1)S(1)} %copy-done.1, bf16[512,4096]{1,0:T(8,128)(2,1)} %reshape.186, bf16[2,4096,256]{2,1,0:T(8,128)(2,1)} %get-tuple-element.12, f32[512,256]{1,0:T(8,128)S(1)} %fusion.9), kind=kOutput, calls=%fused_computation.6 | convolution fusion | flops 2153512960 | bytes 17301504 | tf_op jit(solution)/shard_map/dot_general | solution.py:43
  626.1 7.7 %convert_element_type.179 = bf16[4,64,2,4096]{3,2,1,0:T(2,128)(2,1)} reshape(bf16[512,4096]{1,0:T(8,128)(2,1)} %convolution_convert_fusion.2) | data formatting | bytes 8388608 | tf_op jit(solution)/shard_map/convert_element_type | solution.py:67
  651.3 35.9 %reduce-scatter.3.cloned.1.call-done = bf16[1,64,2,4096]{3,1,2,0:T(8,128)(2,1)} async-done(((bf16[4,64,2,4096]{3,1,2,0:T(8,128)(2,1)}), bf16[1,64,2,4096]{3,1,2,0:T(8,128)(2,1)}) %reduce-scatter.3.cloned.1.call-update) | async-done | bytes 1048592 | tf_op jit(solution)/shard_map/reduce_scatter | solution.py:66
  690.5 10.8 %all-to-all-start.1 = ((bf16[1,64,2,4096]{3,2,0,1:T(2,128)(2,1)}), bf16[1,64,2,4096]{3,2,0,1:T(2,128)(2,1)S(1)}, u32[]{:S(2)}, u32[]{:S(2)}) async-start(bf16[1,64,2,4096]{3,2,0,1:T(2,128)(2,1)} %copy.43), calls=%async_computation.2 | async-start | bytes 2097152 | tf_op jit(solution)/shard_map/all_to_all | solution.py:69
  704.9 24.4 %all-to-all-done.1 = bf16[1,64,2,4096]{3,2,0,1:T(2,128)(2,1)S(1)} async-done(((bf16[1,64,2,4096]{3,2,0,1:T(2,128)(2,1)}), bf16[1,64,2,4096]{3,2,0,1:T(2,128)(2,1)S(1)}, u32[]{:S(2)}, u32[]{:S(2)}) %all-to-all-start.1) | async-done | bytes 1048608 | tf_op jit(solution)/shard_map/all_to_all | solution.py:69
  (97 shorter events, 102.0 us)
Async XLA Ops:
  7.2 695.7 %copy-start = (f32[8,8]{1,0:T(8,128)S(1)}, f32[8,8]{1,0:T(8,128)}, u32[]{:S(2)}) copy-start(f32[8,8]{1,0:T(8,128)} %param.18) | copy-start | bytes 772
  54.1 23.9 %copy-start.1 = (bf16[1,256,4096]{2,1,0:T(8,128)(2,1)S(1)}, bf16[1,256,4096]{2,1,0:T(8,128)(2,1)}, u32[]{:S(2)}) copy-start(bf16[1,256,4096]{2,1,0:T(8,128)(2,1)} %param.24) | copy-start | bytes 6291460
  54.1 24.0 %copy-start.6 = (bf16[1,2,32,2]{2,3,1,0:T(2,128)(2,1)S(1)}, bf16[1,2,32,2]{2,3,1,0:T(2,128)(2,1)}, u32[]{:S(2)}) copy-start(bf16[1,2,32,2]{2,3,1,0:T(2,128)(2,1)} %param.23) | copy-start | bytes 772
  54.1 29.3 %copy-start.7 = (bf16[1,2,32]{2,1,0:T(2,128)(2,1)S(1)}, bf16[1,2,32]{2,1,0:T(2,128)(2,1)}, u32[]{:S(2)}) copy-start(bf16[1,2,32]{2,1,0:T(2,128)(2,1)} %param.25) | copy-start | bytes 388
  54.1 29.4 %copy-start.4 = (s32[8,8]{1,0:T(8,128)S(1)}, s32[8,8]{1,0:T(8,128)}, u32[]{:S(2)}) copy-start(s32[8,8]{1,0:T(8,128)} %param.15) | copy-start | bytes 772
  54.1 39.5 %copy-start.5 = (s32[64]{0:T(128)S(1)}, s32[64]{0:T(128)}, u32[]{:S(2)}) copy-start(s32[64]{0:T(128)} %param.20) | copy-start | bytes 772
  54.1 366.4 %all-to-all-start.2 = ((bf16[4,64,2,4096]{3,2,0,1:T(2,128)(2,1)}), bf16[4,64,2,4096]{3,2,0,1:T(2,128)(2,1)}, u32[]{:S(2)}, u32[]{:S(2)}) async-start(bf16[4,64,2,4096]{3,2,0,1:T(2,128)(2,1)} %copy.44), calls=%async_computation.3 | async-start | bytes 8388608 | tf_op jit(solution)/shard_map/all_to_all | solution.py:96
  72.6 336.1 %collective-permute-start = (bf16[1,2,4096,256]{3,2,1,0:T(8,128)(2,1)}, bf16[1,2,4096,256]{3,2,1,0:T(8,128)(2,1)}, u32[]{:S(2)}, u32[]{:S(2)}) collective-permute-start(bf16[1,2,4096,256]{3,2,1,0:T(8,128)(2,1)} %param.22), channel_id=1, source_target_pairs={{0,128},{128,0},{4,132},{132,4},{8,136},{136,8},{12,140},{140,12},... | collective-permute-start | bytes 12582920 | tf_op jit(solution)/shard_map/ppermute | solution.py:14
  78.0 329.0 %collective-permute-start.2 = (bf16[1,256,4096]{2,1,0:T(8,128)(2,1)S(1)}, bf16[1,256,4096]{2,1,0:T(8,128)(2,1)}, u32[]{:S(2)}, u32[]{:S(2)}) collective-permute-start(bf16[1,256,4096]{2,1,0:T(8,128)(2,1)S(1)} %copy-done.1), channel_id=1, source_target_pairs={{0,128},{128,0},{4,132},{132,4},{8,136},{136,8},{12,140},{140,12},... | collective-permute-start | bytes 6291464 | tf_op jit(solution)/shard_map/ppermute | solution.py:14
  78.2 294.2 %collective-permute-start.1 = (bf16[1,2,32,2]{2,3,1,0:T(2,128)(2,1)S(1)}, bf16[1,2,32,2]{2,3,1,0:T(2,128)(2,1)S(1)}, u32[]{:S(2)}, u32[]{:S(2)}) collective-permute-start(bf16[1,2,32,2]{2,3,1,0:T(2,128)(2,1)S(1)} %copy-done.6), channel_id=1, source_target_pairs={{0,128},{128,0},{4,132},{132,4},{8,136},{136,8},{12,140},{140,12},... | collective-permute-start | bytes 776 | tf_op jit(solution)/shard_map/ppermute | solution.py:14
  83.4 288.4 %collective-permute-start.3 = (bf16[1,2,32]{2,1,0:T(2,128)(2,1)S(1)}, bf16[1,2,32]{2,1,0:T(2,128)(2,1)S(1)}, u32[]{:S(2)}, u32[]{:S(2)}) collective-permute-start(bf16[1,2,32]{2,1,0:T(2,128)(2,1)S(1)} %copy-done.7), channel_id=1, source_target_pairs={{0,128},{128,0},{4,132},{132,4},{8,136},{136,8},{12,140},{140,12},... | collective-permute-start | bytes 392 | tf_op jit(solution)/shard_map/ppermute | solution.py:14
  116.8 10.2 %copy-start.9 = (s32[64]{0:T(128)S(1)}, s32[64]{0:T(128)}, u32[]{:S(2)}) copy-start(s32[64]{0:T(128)} %param.21) | copy-start | bytes 772
  407.0 2.9 copy-start.2
  420.5 170.4 %all-to-all-start = ((bf16[4,64,2,4096]{3,2,0,1:T(2,128)(2,1)}), bf16[4,64,2,4096]{3,2,0,1:T(2,128)(2,1)}, u32[]{:S(2)}, u32[]{:S(2)}) async-start(bf16[4,64,2,4096]{3,2,0,1:T(2,128)(2,1)} %copy.39), calls=%async_computation | async-start | bytes 8388608 | tf_op jit(solution)/shard_map/all_to_all | solution.py:96
  496.0 144.9 %reduce-scatter.5.cloned.1.call-start = ((), (), s32[]{:S(2)}) async-start(), calls=%async_computation.7 | async-start | bytes 5242880 | tf_op jit(solution)/shard_map/reduce_scatter | solution.py:66
  546.4 140.7 %reduce-scatter.3.cloned.1.call-start = ((), (), s32[]{:S(2)}) async-start(), calls=%async_computation.6 | async-start | bytes 5242880 | tf_op jit(solution)/shard_map/reduce_scatter | solution.py:66
  640.8 60.4 %copy-start.3 = (s32[8,8]{1,0:T(8,128)S(1)}, s32[8,8]{1,0:T(8,128)}, u32[]{:S(2)}) copy-start(s32[8,8]{1,0:T(8,128)} %param.16) | copy-start | bytes 772
  640.8 62.3 %copy-start.8 = (f32[8,8]{1,0:T(8,128)S(1)}, f32[8,8]{1,0:T(8,128)}, u32[]{:S(2)}) copy-start(f32[8,8]{1,0:T(8,128)} %param.17) | copy-start | bytes 772
  644.2 46.3 %all-to-all-start.3 = ((bf16[1,64,2,4096]{3,2,0,1:T(2,128)(2,1)}), bf16[1,64,2,4096]{3,2,0,1:T(2,128)(2,1)S(1)}, u32[]{:S(2)}, u32[]{:S(2)}) async-start(bf16[1,64,2,4096]{3,2,0,1:T(2,128)(2,1)} %copy.48), calls=%async_computation.5 | async-start | bytes 2097152 | tf_op jit(solution)/shard_map/all_to_all | solution.py:69
  690.5 38.9 %all-to-all-start.1 = ((bf16[1,64,2,4096]{3,2,0,1:T(2,128)(2,1)}), bf16[1,64,2,4096]{3,2,0,1:T(2,128)(2,1)S(1)}, u32[]{:S(2)}, u32[]{:S(2)}) async-start(bf16[1,64,2,4096]{3,2,0,1:T(2,128)(2,1)} %copy.43), calls=%async_computation.2 | async-start | bytes 2097152 | tf_op jit(solution)/shard_map/all_to_all | solution.py:69
Sparse Core Ops, SparseCore 0:
  546.6 49.7 reduce-scatter.4
  640.9 46.1 reduce-scatter.2
where the time goes:
time: 749 us; the launch traced here: 738 us
  waiting for transfers between devices  348 us (46%)
  local copies, waits for them, and re-layouts  148 us (20%)
  starting transfers between devices  123 us (16%)
  matrix products  40.9 us (5%)
  blocking collectives  40.4 us (5%)
  other arithmetic  22.3 us (3%)
  between operations  15.4 us (2%)
    ppermute x4, waiting for transfers between devices, partner(): return lax.ppermute(block, axis, route)  244 us
    all_to_all x2, starting transfers between devices, decode_step(): lax.all_to_all(outgoing, 'expert', split_axis=1, concat_axis=1, tiled=True)  93.9 us
    all_to_all x2, waiting for transfers between devices, decode_step(): lax.all_to_all(outgoing, 'expert', split_axis=1, concat_axis=1, tiled=True)  44.4 us
    mul x6, local copies, waits for them, and re-layouts, dequantize(): scaled = blocked * scales.astype(jnp.float32)[..., :, None, :, None]  39 us
    reduce_scatter x2, waiting for transfers between devices, finish(): lax.psum_scatter(partial_terms.astype(jnp.bfloat16), 'replica', scatter_d...  35.9 us
    reshape x4, local copies, waits for them, and re-layouts, decode_step(): outgoing.astype(jnp.bfloat16).reshape(copies, experts, capacity, features)  35.8 us
    convert_element_type x4, local copies, waits for them, and re-layouts, finish(): partial_terms.astype(jnp.bfloat16)  29.4 us
    all_to_all x2, waiting for transfers between devices, finish(): lax.all_to_all(summed, 'expert', split_axis=1, concat_axis=1, tiled=True)  24.4 us
  transfers between devices with their start and end apart: 10, of which 4 were waited for; matrix products, arithmetic and copies ran while one was open for 25% of the time, Pallas kernels for 0%

commit v1 on v0

v1 whole, which is shorter than its diff:
```python
import jax
import jax.numpy as jnp
from jax import lax
from jax.experimental import pallas as pl
from jax.experimental.pallas import tpu as pltpu
from jax.sharding import PartitionSpec as P


BF16 = jnp.bfloat16
F32 = jnp.float32
I32 = jnp.int32
TOK = 8
CAP = 2
LANES = 128
PLANE = 8
VMEM = pltpu.VMEM
SMEM = pltpu.SMEM


def iota(shape, dim):
    return lax.broadcasted_iota(I32, shape, dim)


def vspec():
    return pl.BlockSpec(memory_space=VMEM)


def sspec():
    return pl.BlockSpec(memory_space=SMEM)


def gate_up_dequant(values, scale_rows):
    _, features, width = values.shape
    rows = features // 4
    blocks = rows // LANES

    def kernel(v_ref, s_ref, o_ref):
        wide = v_ref[0].astype(F32).reshape(blocks, LANES, width)
        o_ref[0] = (wide * s_ref[0][:, None, :]).reshape(rows, width).astype(BF16)

    return pl.pallas_call(
        kernel,
        grid=(2, 4),
        in_specs=[
            pl.BlockSpec((1, rows, width), lambda g, i: (g, i, 0)),
            pl.BlockSpec((1, blocks, width), lambda g, i: (g, i, 0)),
        ],
        out_specs=pl.BlockSpec((1, rows, width), lambda g, i: (g, i, 0)),
        out_shape=jax.ShapeDtypeStruct(values.shape, BF16),
        name="gate_up_dequant",
    )(values, scale_rows)


def down_dequant(values, scale_rows, order):
    height, features = values.shape
    copies = order.shape[0]
    width = features // copies
    blocks = scale_rows.shape[0]

    def kernel(order_ref, v_ref, s_ref, o_ref):
        wide = v_ref[...].astype(F32).reshape(blocks, height // blocks, width)
        o_ref[0] = (wide * s_ref[...][:, None, :]).reshape(height, width).astype(BF16)

    return pl.pallas_call(
        kernel,
        grid_spec=pltpu.PrefetchScalarGridSpec(
            num_scalar_prefetch=1,
            grid=(copies,),
            in_specs=[
                pl.BlockSpec((height, width), lambda k, o: (0, o[k])),
                pl.BlockSpec((blocks, width), lambda k, o: (0, o[k])),
            ],
            out_specs=pl.BlockSpec((1, height, width), lambda k, o: (k, 0, 0)),
        ),
        out_shape=jax.ShapeDtypeStruct((copies, height, width), BF16),
        name="down_dequant",
    )(order, values, scale_rows)


def norm_and_pack(hidden, ids, gain):
    rows, features = hidden[0].shape

    def kernel(h0, h1, i0, i1, g_ref, o_ref):
        for at, h_ref, i_ref in ((0, h0, i0), (rows, h1, i1)):
            wide = h_ref[...].astype(F32)
            inverse = lax.rsqrt(jnp.mean(wide * wide, axis=-1, keepdims=True) + 1e-06)
            o_ref[at : at + rows, :features] = (wide * inverse * g_ref[...]).astype(BF16)
            o_ref[at : at + rows, features:] = i_ref[...]

    return pl.pallas_call(
        kernel,
        in_specs=[vspec()] * 5,
        out_specs=vspec(),
        out_shape=jax.ShapeDtypeStruct((2 * rows, features + LANES), BF16),
        name="norm_and_pack",
    )(hidden[0], hidden[1], ids[0], ids[1], gain)


def select_rows(gathered, my_expert):
    both, packed = gathered.shape
    features = packed - LANES
    rows = both // 2
    kept = rows // TOK * CAP

    def kernel(e_ref, g_ref, *o_refs):
        mine = e_ref[0].astype(F32)
        r, q = iota((rows, rows), 0), iota((rows, rows), 1)
        before = jnp.where(((r >> 3) == (q >> 3)) & (q < r), 1.0, 0.0).astype(BF16)
        row, col = iota((rows, kept), 0), iota((rows, kept), 1)

        def of_step(step, start, size):
            part = g_ref[:, start : start + size].reshape(rows // TOK, 2, TOK, size)
            return part[:, step].reshape(rows, size)

        for step, o_ref in enumerate(o_refs):
            ids = of_step(step, features, LANES).astype(F32)
            hit = jnp.max(jnp.where(ids == mine, 1.0, 0.0), axis=1, keepdims=True)
            hits = jnp.broadcast_to(hit, (rows, kept))
            rank = jnp.dot(before, hits.astype(BF16), preferred_element_type=F32)
            chosen = ((row >> 3) == (col >> 1)) & (rank == (col & 1).astype(F32)) & (hits > 0.5)
            picking = jnp.where(chosen, 1.0, 0.0).astype(BF16)
            for at in range(0, features, 1024):
                o_ref[:, at : at + 1024] = lax.dot_general(
                    picking,
                    of_step(step, at, 1024),
                    (((0,), (0,)), ((), ())),
                    preferred_element_type=F32,
                ).astype(BF16)

    shape = jax.ShapeDtypeStruct((kept, features), BF16)
    return pl.pallas_call(
        kernel,
        in_specs=[sspec(), vspec()],
        out_specs=[vspec()] * 2,
        out_shape=[shape] * 2,
        name="select_rows",
    )(my_expert, gathered)


def gate_up(pieces, weights, columns):
    copies = len(pieces)
    rows, features = pieces[0].shape
    width = weights.shape[2]

    def kernel(c_ref, *refs):
        x_refs, w_ref, o_ref, x_all = refs[:copies], refs[copies], refs[copies + 1], refs[copies + 2]
        for k in range(copies):
            start = pl.multiple_of(c_ref[k] * rows, rows)
            x_all[pl.ds(start, rows), :] = x_refs[k][...]
        gate = jnp.dot(x_all[...], w_ref[0], preferred_element_type=F32)
        up = jnp.dot(x_all[...], w_ref[1], preferred_element_type=F32)
        o_ref[...] = (gate / (1.0 + jnp.exp(-gate)) * up).astype(BF16)

    return pl.pallas_call(
        kernel,
        in_specs=[sspec()] + [vspec()] * (copies + 1),
        out_specs=vspec(),
        out_shape=jax.ShapeDtypeStruct((copies * rows, width), BF16),
        scratch_shapes=[pltpu.VMEM((copies * rows, features), BF16)],
        name="gate_up",
    )(columns, *pieces, weights)


def down(inner, weights):
    copies = len(inner)
    rows, _ = inner[0].shape
    kept = rows // copies
    width = weights[0].shape[1]

    def kernel(*refs):
        i_refs, w_refs, o_ref = refs[:copies], refs[copies : 2 * copies], refs[2 * copies]
        r, q = iota((rows, rows), 0), iota((rows, rows), 1)
        source = ((r >> 1) & 3) * kept + ((r >> 3) << 1) + (r & 1)
        order = jnp.where(q == source, 1.0, 0.0).astype(BF16)
        total = jnp.zeros((rows, width), F32)
        for i_ref, w_ref in zip(i_refs, w_refs):
            placed = jnp.dot(order, i_ref[...], preferred_element_type=F32).astype(BF16)
            total = total + jnp.dot(placed, w_ref[...], preferred_element_type=F32)
        o_ref[...] = total.astype(BF16)

    return pl.pallas_call(
        kernel,
        in_specs=[vspec()] * (2 * copies),
        out_specs=vspec(),
        out_shape=jax.ShapeDtypeStruct((rows, width), BF16),
        name="down",
    )(*inner, *weights)


def mixing_tables(packed, plane_experts):
    tokens, top = packed.shape[0], packed.shape[1] // 4
    places = plane_experts.shape[1]

    def kernel(p_ref, e_ref, *outs):
        at = e_ref[...].astype(F32)
        r, q = iota((tokens, tokens), 0), iota((tokens, tokens), 1)
        before = jnp.where(((r >> 3) == (q >> 3)) & (q < r), 1.0, 0.0).astype(BF16)
        row, col = iota((tokens, places), 0), iota((tokens, places), 1)
        for step in range(2):
            hit = jnp.zeros((tokens, places), F32)
            weight = jnp.zeros((tokens, places), F32)
            for k in range(top):
                lane = step * 2 * top + k
                same = p_ref[:, lane : lane + 1] == at
                hit = hit + jnp.where(same, 1.0, 0.0)
                weight = weight + jnp.where(same, p_ref[:, lane + top : lane + top + 1], 0.0)
            rank = jnp.dot(before, hit.astype(BF16), preferred_element_type=F32)
            here = (((row >> 3) & 3) == ((col >> 1) & 3)) & (rank == (col & 1).astype(F32))
            kept = jnp.where(here, weight, 0.0)
            high = kept.astype(BF16)
            outs[2 * step][...] = high
            outs[2 * step + 1][...] = (kept - high.astype(F32)).astype(BF16)

    shape = jax.ShapeDtypeStruct((tokens, places), BF16)
    return pl.pallas_call(
        kernel,
        in_specs=[vspec(), vspec()],
        out_specs=[vspec()] * 4,
        out_shape=[shape] * 4,
        name="mixing_tables",
    )(packed, plane_experts)


def combine(returned, tables, copies):
    members, levels, rows, width = returned[0].shape

    def kernel(r0, r1, h0, l0, h1, l1, o_ref):
        for step, (r_ref, h_ref, l_ref) in enumerate(((r0, h0, l0), (r1, h1, l1))):
            for level in range(levels):
                found = r_ref[:, level].reshape(members * rows, width)
                at = slice(level * copies * TOK, (level + 1) * copies * TOK)
                total = jnp.dot(h_ref[at, :], found, preferred_element_type=F32) + jnp.dot(
                    l_ref[at, :], found, preferred_element_type=F32
                )
                o_ref[level, :, step] = total.astype(BF16).reshape(copies, TOK, width)

    return pl.pallas_call(
        kernel,
        in_specs=[vspec()] * 6,
        out_specs=vspec(),
        out_shape=jax.ShapeDtypeStruct((levels, copies, 2, TOK, width), BF16),
        name="combine",
    )(returned[0], returned[1], *tables)


def add_levels(parts):
    levels, rows, width = parts.shape

    def kernel(p_ref, o_ref):
        total = p_ref[0].astype(F32)
        for level in range(1, levels):
            total = total + p_ref[level].astype(F32)
        o_ref[...] = total.astype(BF16)

    return pl.pallas_call(
        kernel,
        in_specs=[vspec()],
        out_specs=vspec(),
        out_shape=jax.ShapeDtypeStruct((rows, width), BF16),
        name="add_levels",
    )(parts)


def shifted(block, shift):
    copies = lax.axis_size("replica")
    return lax.ppermute(block, "replica", [(i, (i + shift) % copies) for i in range(copies)])


def level_groups():
    experts = lax.axis_size("expert")
    return [list(range(member, experts, PLANE)) for member in range(PLANE)]


def plane_groups():
    experts = lax.axis_size("expert")
    return [list(range(at, at + PLANE)) for at in range(0, experts, PLANE)]


def swapped(block):
    experts = lax.axis_size("expert")
    half = experts // 2
    return lax.ppermute(block, "expert", [(i, (i + half) % experts) for i in range(experts)])


def layer(
    hidden_first,
    hidden_second,
    routes_first,
    routes_second,
    mixing_first,
    mixing_second,
    norm_gain,
    expert_owner,
    swap_flags,
    gate_up_values,
    gate_up_scales,
    down_values,
    down_scales,
):
    experts = lax.axis_size("expert")
    copies = lax.axis_size("replica")
    my_slot = lax.axis_index("expert")
    my_copy = lax.axis_index("replica")
    features = hidden_first.shape[1]
    slot_ids = jnp.arange(experts, dtype=I32)

    current = (gate_up_values, gate_up_scales, down_values, down_scales)
    incoming = []
    for piece in current:
        incoming.append(swapped(piece))
    flagged = jnp.sum(jnp.where(slot_ids == my_slot, swap_flags, 0)) == 1

    expert_at = jnp.sum(
        jnp.where(expert_owner[:, None] == slot_ids[None, :], slot_ids[:, None], 0), axis=0
    )
    my_expert = jnp.sum(jnp.where(expert_owner == my_slot, slot_ids, 0)).reshape(1)
    hops = jnp.arange(copies, dtype=I32)
    ahead = (my_copy + hops) % copies
    behind = (my_copy - hops + copies) % copies

    ids = [
        jnp.pad(routes.astype(BF16), ((0, 0), (0, LANES - routes.shape[1])), constant_values=-1)
        for routes in (routes_first, routes_second)
    ]
    packs = norm_and_pack((hidden_first, hidden_second), ids, norm_gain.reshape(1, features))
    column = lax.all_gather(packs, "expert", axis=0, tiled=True, axis_index_groups=level_groups())
    gathered = lax.all_gather(
        column, "expert", axis=0, tiled=True, axis_index_groups=plane_groups()
    )

    gate_up_rows = jnp.repeat(gate_up_scales[0].astype(F32), LANES, axis=-1)
    down_rows = jnp.repeat(down_scales[0].astype(F32), LANES, axis=-1)
    down_sent = down_dequant(down_values[0], down_rows, ahead)
    down_weights = [down_sent[0]] + [shifted(down_sent[k], k) for k in range(1, copies)]
    gate_up_weights = gate_up_dequant(gate_up_values[0], gate_up_rows)
    picks = jnp.concatenate(
        [
            routes_first.astype(F32),
            mixing_first,
            routes_second.astype(F32),
            mixing_second,
        ],
        axis=1,
    )
    all_picks = lax.all_gather(picks, "replica", axis=0, tiled=True)
    all_picks = lax.all_gather(
        all_picks, "expert", axis=0, tiled=True, axis_index_groups=level_groups()
    )
    first = my_slot // PLANE * PLANE
    plane_experts = lax.dynamic_slice(expert_at, (first,), (PLANE,))
    plane_experts = jnp.repeat(plane_experts, copies * CAP).reshape(1, PLANE * copies * CAP)
    tables = mixing_tables(all_picks, plane_experts)

    chosen_rows = select_rows(gathered, my_expert)
    returned = []
    for step in range(2):
        own_rows = chosen_rows[step]
        pieces = [own_rows] + [shifted(own_rows, k) for k in range(1, copies)]
        inner = gate_up(pieces, gate_up_weights, behind)
        inners = [inner] + [shifted(inner, k) for k in range(1, copies)]
        results = down(inners, down_weights)
        back = lax.all_to_all(
            results.reshape(PLANE, experts // PLANE, copies * CAP, features // copies),
            "expert",
            split_axis=0,
            concat_axis=0,
            tiled=True,
            axis_index_groups=plane_groups(),
        )
        returned.append(back)

    mixed = combine(returned, tables, copies)
    levels = lax.all_to_all(
        mixed.reshape(experts // PLANE, copies * 2 * TOK, features // copies),
        "expert",
        split_axis=0,
        concat_axis=0,
        tiled=True,
        axis_index_groups=level_groups(),
    )
    summed = add_levels(levels).reshape(copies, 2 * TOK, features // copies)
    spread = lax.all_to_all(summed, "replica", split_axis=0, concat_axis=0, tiled=True)
    outputs = tuple(
        spread[:, step * TOK : (step + 1) * TOK].transpose(1, 0, 2).reshape(TOK, features)
        for step in range(2)
    )
    incoming = lax.optimization_barrier((*incoming, mixed))[: len(current)]
    moved = tuple(
        jnp.where(flagged, fresh, stale) for fresh, stale in zip(incoming, current)
    )
    return outputs + moved


def solution(mesh):
    tokens = P(("expert", "replica"), None)
    weights = (
        P("expert", None, None, "replica"),
        P("expert", None, None, "replica"),
        P("expert", "replica", None),
        P("expert", "replica", None),
    )
    return jax.shard_map(
        layer,
        mesh=mesh,
        in_specs=(tokens,) * 6 + (P(),) * 3 + weights,
        out_specs=(tokens,) * 2 + weights,
        check_vma=False,
    )
```

time: 749 us -> 402 us (0.54)
  waiting for transfers between devices: 348 us -> 195 us
  local copies, waits for them, and re-layouts: 148 us -> 10.4 us
  starting transfers between devices: 123 us -> 56.2 us
  Pallas kernels: 0 us -> 52 us
  matrix products: 40.9 us -> 0 us
  blocking collectives: 40.4 us -> 58 us
  other arithmetic: 22.3 us -> 9 us
    ppermute x4 -> x19, waiting for transfers between devices: 244 us -> 79.8 us  [the longest x15 79.8 us: shifted(): lax.ppermute(block, 'replica', [(i, (i + shift) % copies) for i in range(...]
    all_to_all x4, starting transfers between devices: 112 us -> 19.4 us  [the longest x2 11.5 us: layer(): lax.all_to_all(results.reshape(PLANE, experts // PLANE, copies * CAP, fea...]
    all_gather x0 -> x2, waiting for transfers between devices: none -> 92.1 us  [the longest x1 54.7 us: layer(): lax.all_gather(column, 'expert', axis=0, tiled=True, axis_index_groups=pl...]
    pallas_call x0 -> x11, Pallas kernels: none -> 52 us  [the longest x2 13.7 us: gate_up(): pl.pallas_call(kernel, in_specs=[sspec()] + [vspec()] * (copies + 1), out...]
    reshape x8 -> x1, local copies, waits for them, and re-layouts: 51.5 us -> 0.69 us  [layer(): gate_up_rows = jnp.repeat(gate_up_scales[0].astype(F32), LANES, axis=-1)]
    all_to_all x4, waiting for transfers between devices: 68.9 us -> 23.3 us  [the longest x1 19 us: layer(): lax.all_to_all(mixed.reshape(experts // PLANE, copies * 2 * TOK, features...]
    dot_general x10 -> x0, matrix products: 40.9 us -> none  [the longest x2 23.3 us: expert_partial(): jnp.dot(inner_act, down_proj, preferred_element_type=jnp.float32)]
    mul x6 -> x0, local copies, waits for them, and re-layouts: 39 us -> none  [dequantize(): scaled = blocked * scales.astype(jnp.float32)[..., :, None, :, None]]
  transfers between devices with their start and end apart: 10 -> 25, of which waited for: 4 -> 15; matrix products, arithmetic and copies ran while one was open for 25% -> 3% of each run, Pallas kernels for 0% -> 12%
where the time goes in v1:
time: 402 us; the launch traced here: 396 us
  waiting for transfers between devices  195 us (49%)
  blocking collectives  58 us (14%)
  starting transfers between devices  56.2 us (14%)
  Pallas kernels  52 us (13%)
  between operations  14.8 us (4%)
  local copies, waits for them, and re-layouts  10.4 us (3%)
  other arithmetic  9 us (2%)
    ppermute x15, waiting for transfers between devices, shifted(): lax.ppermute(block, 'replica', [(i, (i + shift) % copies) for i in range(...  79.8 us
    all_gather x1, waiting for transfers between devices, layer(): lax.all_gather(column, 'expert', axis=0, tiled=True, axis_index_groups=pl...  54.7 us
    all_gather x1, blocking collectives, layer(): lax.all_gather(all_picks, 'expert', axis=0, tiled=True, axis_index_groups...  48.6 us
    all_gather x1, waiting for transfers between devices, layer(): lax.all_gather(packs, 'expert', axis=0, tiled=True, axis_index_groups=lev...  37.4 us
    ppermute x15, starting transfers between devices, shifted(): lax.ppermute(block, 'replica', [(i, (i + shift) % copies) for i in range(...  22.5 us
    all_to_all x1, waiting for transfers between devices, layer(): lax.all_to_all(mixed.reshape(experts // PLANE, copies * 2 * TOK, features...  19 us
    ppermute x4, starting transfers between devices, swapped(): lax.ppermute(block, 'expert', [(i, (i + half) % experts) for i in range(e...  14.2 us
    pallas_call x2, Pallas kernels, gate_up(): pl.pallas_call(kernel, in_specs=[sspec()] + [vspec()] * (copies + 1), out...  13.7 us
  transfers between devices with their start and end apart: 25, of which 15 were waited for; matrix products, arithmetic and copies ran while one was open for 3% of the time, Pallas kernels for 12%

profile of v1, /device:TPU:1, one launch (start us, length us, event | category | flops | bytes accessed | tf_op | source)
XLA Modules:
  0.0 395.7 jit_solution(1310877849374416209)
XLA Ops:
  10.9 37.4 %all-gather.3.cloned.1.call-done = bf16[128,4224]{1,0:T(8,128)(2,1)} async-done(((bf16[16,4224]{1,0:T(8,128)(2,1)}), bf16[128,4224]{1,0:T(8,128)(2,1)}) %all-gather.3.cloned.1.call-update) | async-done | bytes 1081360 | tf_op jit(solution)/shard_map/all_gather | solution.py:326
  52.9 54.7 %all-gather.5.cloned.1.call-done.g_ref = bf16[1024,4224]{1,0:T(8,128)(2,1)} async-done(((bf16[128,4224]{1,0:T(8,128)(2,1)}), bf16[1024,4224]{1,0:T(8,128)(2,1)}) %all-gather.5.cloned.1.call-update) | async-done | bytes 8650768 | tf_op jit(solution)/shard_map/all_gather | solution.py:327
  107.6 7.3 %select_rows.1 = (bf16[128,4096]{1,0:T(8,128)(2,1)}, bf16[128,4096]{1,0:T(8,128)(2,1)}) custom-call(s32[1]{0:T(128)} %bitcast.e_ref, bf16[1024,4224]{1,0:T(8,128)(2,1)} %all-gather.5.cloned.1.call-done.g_ref), custom_call_target="tpu_custom_call" | custom-call | tf_op jit(solution)/shard_map/select_rows/pallas_call | solution.py:131
  120.3 4.6 %down_dequant.1 = bf16[4,256,1024]{2,1,0:T(8,128)(2,1)} custom-call(s32[4]{0:T(128)} %and_select_fusion.order_ref, bf16[256,4096]{1,0:T(8,128)(2,1)} %bitcast.34, f32[2,4096]{1,0:T(2,128)} %bitcast.39), custom_call_target="tpu_custom_call" | custom-call | tf_op jit(solution)/shard_map/down_dequant/pallas_call | solution.py:64
  128.0 13.2 %collective-permute-done.10.refs_2_ = bf16[128,4096]{1,0:T(8,128)(2,1)S(1)} collective-permute-done((bf16[128,4096]{1,0:T(8,128)(2,1)}, bf16[128,4096]{1,0:T(8,128)(2,1)S(1)}, u32[]{:S(2)}, u32[]{:S(2)}) %collective-permute-start.10) | collective-permute-done | bytes 1048608 | tf_op jit(solution)/shard_map/ppermute | solution.py:266
  143.9 19.8 %collective-permute-done.11.refs_3_ = bf16[128,4096]{1,0:T(8,128)(2,1)S(1)} collective-permute-done((bf16[128,4096]{1,0:T(8,128)(2,1)}, bf16[128,4096]{1,0:T(8,128)(2,1)S(1)}, u32[]{:S(2)}, u32[]{:S(2)}) %collective-permute-start.11) | collective-permute-done | bytes 1048608 | tf_op jit(solution)/shard_map/ppermute | solution.py:266
  168.2 6.8 %gate_up_dequant.1.refs_4_ = bf16[2,4096,256]{2,1,0:T(8,128)(2,1)} custom-call(bf16[2,4096,256]{2,1,0:T(8,128)(2,1)} %bitcast.33, f32[2,32,256]{2,1,0:T(8,128)} %reshape.49.s_ref), custom_call_target="tpu_custom_call" | custom-call | tf_op jit(solution)/shard_map/gate_up_dequant/pallas_call | solution.py:41
  175.5 6.9 %gate_up.3.refs_0_ = bf16[512,256]{1,0:T(8,128)(2,1)} custom-call(s32[4]{0:T(128)} %and_select_fusion.1.c_ref, bf16[128,4096]{1,0:T(8,128)(2,1)} %get-tuple-element.17.refs_0_, bf16[128,4096]{1,0:T(8,128)(2,1)} %collective-permute-done.9.refs_1_, bf16[128,4096]{1,0:T(8,128)(2,1)} %copy-done.6, bf16[128,4096]{1,0:T(8,128)(2,1)} %copy-done.7, ...), custom_call_target="tpu_custom_call" | custom-call | tf_op jit(solution)/shard_map/gate_up/pallas_call | solution.py:154
  199.0 5.5 %collective-permute-start.17 = (bf16[1,256,4096]{2,1,0:T(8,128)(2,1)S(1)}, bf16[1,256,4096]{2,1,0:T(8,128)(2,1)}, u32[]{:S(2)}, u32[]{:S(2)}) collective-permute-start(bf16[1,256,4096]{2,1,0:T(8,128)(2,1)S(1)} %copy-done.1), channel_id=1, source_target_pairs={{0,128},{4,132},{8,136},{12,140},{16,144},{20,148},{24,152},{28,15... | collective-permute-start | bytes 6291464 | tf_op jit(solution)/shard_map/ppermute | solution.py:282
  204.4 4.9 %down.3 = bf16[512,1024]{1,0:T(8,128)(2,1)} custom-call(bf16[512,256]{1,0:T(8,128)(2,1)} %gate_up.3.refs_0_, bf16[512,256]{1,0:T(8,128)(2,1)} %copy-done.8, bf16[512,256]{1,0:T(8,128)(2,1)} %copy-done.9, bf16[512,256]{1,0:T(8,128)(2,1)} %copy-done.10, bf16[256,1024]{1,0:T(8,128)(2,1)} %get-tuple-element.29.refs_4_, bf16[256,1024]{1,0:T(8,128)(2,1)} %copy-done.4, ...), custom_call_target="tpu_custom_call" | custom-call | tf_op jit(solution)/shard_map/down/pallas_call | solution.py:181
  209.3 5.8 %all-to-all-start.1 = ((bf16[8,8,8,1024]{3,2,1,0:T(8,128)(2,1)}), bf16[8,8,8,1024]{3,2,1,0:T(8,128)(2,1)S(1)}, u32[]{:S(2)}, u32[]{:S(2)}) async-start(bf16[8,8,8,1024]{3,2,1,0:T(8,128)(2,1)} %bitcast.37), calls=%async_computation.1 | async-start | bytes 2097152 | tf_op jit(solution)/shard_map/all_to_all | solution.py:362
  215.1 5.1 %collective-permute-done.refs_1_ = bf16[128,4096]{1,0:T(8,128)(2,1)} collective-permute-done((bf16[128,4096]{1,0:T(8,128)(2,1)}, bf16[128,4096]{1,0:T(8,128)(2,1)}, u32[]{:S(2)}, u32[]{:S(2)}) %collective-permute-start) | collective-permute-done | bytes 1048608 | tf_op jit(solution)/shard_map/ppermute | solution.py:266
  220.2 22.2 %collective-permute-done.1.refs_2_ = bf16[128,4096]{1,0:T(8,128)(2,1)} collective-permute-done((bf16[128,4096]{1,0:T(8,128)(2,1)}, bf16[128,4096]{1,0:T(8,128)(2,1)}, u32[]{:S(2)}, u32[]{:S(2)}) %collective-permute-start.1) | collective-permute-done | bytes 1048608 | tf_op jit(solution)/shard_map/ppermute | solution.py:266
  242.4 6.8 %gate_up.2.refs_0_ = bf16[512,256]{1,0:T(8,128)(2,1)} custom-call(s32[4]{0:T(128)} %and_select_fusion.1.c_ref, bf16[128,4096]{1,0:T(8,128)(2,1)} %get-tuple-element.16.refs_0_, bf16[128,4096]{1,0:T(8,128)(2,1)} %collective-permute-done.refs_1_, bf16[128,4096]{1,0:T(8,128)(2,1)} %collective-permute-done.1.refs_2_, ...), custom_call_target="tpu_custom_call" | custom-call | tf_op jit(solution)/shard_map/gate_up/pallas_call | solution.py:154
  254.0 4.3 %collective-permute-done.3.refs_1_ = bf16[512,256]{1,0:T(8,128)(2,1)S(1)} collective-permute-done((bf16[512,256]{1,0:T(8,128)(2,1)}, bf16[512,256]{1,0:T(8,128)(2,1)S(1)}, u32[]{:S(2)}, u32[]{:S(2)}) %collective-permute-start.3) | collective-permute-done | bytes 262176 | tf_op jit(solution)/shard_map/ppermute | solution.py:266
  258.3 7.2 %collective-permute-done.4.refs_2_ = bf16[512,256]{1,0:T(8,128)(2,1)} collective-permute-done((bf16[512,256]{1,0:T(8,128)(2,1)}, bf16[512,256]{1,0:T(8,128)(2,1)}, u32[]{:S(2)}, u32[]{:S(2)}) %collective-permute-start.4) | collective-permute-done | bytes 262176 | tf_op jit(solution)/shard_map/ppermute | solution.py:266
  265.5 4.9 %down.2 = bf16[512,1024]{1,0:T(8,128)(2,1)} custom-call(bf16[512,256]{1,0:T(8,128)(2,1)} %gate_up.2.refs_0_, bf16[512,256]{1,0:T(8,128)(2,1)} %copy-done.11, bf16[512,256]{1,0:T(8,128)(2,1)} %collective-permute-done.4.refs_2_, bf16[512,256]{1,0:T(8,128)(2,1)} %collective-permute-done.5.refs_3_, bf16[256,1024]{1,0:T(8,128)(2,1)} %get-tuple-element.29.refs_4_, ...), custom_call_target="tpu_custom_call" | custom-call | tf_op jit(solution)/shard_map/down/pallas_call | solution.py:181
  270.4 5.7 %all-to-all-start = ((bf16[8,8,8,1024]{3,2,1,0:T(8,128)(2,1)}), bf16[8,8,8,1024]{3,2,1,0:T(8,128)(2,1)}, u32[]{:S(2)}, u32[]{:S(2)}) async-start(bf16[8,8,8,1024]{3,2,1,0:T(8,128)(2,1)} %bitcast.36), calls=%async_computation | async-start | bytes 2097152 | tf_op jit(solution)/shard_map/all_to_all | solution.py:362
  276.0 5.5 %collective-permute-start.16 = (bf16[1,2,32,2]{2,3,1,0:T(2,128)(2,1)S(1)}, bf16[1,2,32,2]{2,3,1,0:T(2,128)(2,1)S(1)}, u32[]{:S(2)}, u32[]{:S(2)}) collective-permute-start(bf16[1,2,32,2]{2,3,1,0:T(2,128)(2,1)S(1)} %copy-done.14), channel_id=1, source_target_pairs={{0,128},{4,132},{8,136},{12,140},{16,144},{20,148},{24,152},{28,15... | collective-permute-start | bytes 776 | tf_op jit(solution)/shard_map/ppermute | solution.py:282
  283.8 9.4 %all_gather.14 = f32[32,32]{1,0:T(8,128)S(1)} all-gather(f32[8,32]{1,0:T(8,128)S(1)} %pad_maximum_fusion), channel_id=1, replica_groups=mesh['expert'=64,'replica'=4] {'replica'}, dimensions={0}, use_global_device_ids=true | all-gather | bytes 5120 | tf_op jit(solution)/shard_map/all_gather | solution.py:345
  293.2 48.6 %all_gather.15.p_ref = f32[256,32]{1,0:T(8,128)} all-gather(f32[32,32]{1,0:T(8,128)S(1)} %all_gather.14), channel_id=1, replica_groups={{0,32,64,96,128,160,192,224},{4,36,68,100,132,164,196,228},{8,40,72,104..., dimensions={0}, use_global_device_ids=true | all-gather | bytes 36864 | tf_op jit(solution)/shard_map/all_gather | solution.py:346
  348.0 4.3 %all-to-all-start.2 = ((bf16[8,64,1024]{2,1,0:T(8,128)(2,1)}), bf16[8,64,1024]{2,1,0:T(8,128)(2,1)S(1)}, u32[]{:S(2)}, u32[]{:S(2)}) async-start(bf16[8,64,1024]{2,1,0:T(8,128)(2,1)} %bitcast.35), calls=%async_computation.2 | async-start | bytes 2097152 | tf_op jit(solution)/shard_map/all_to_all | solution.py:373
  357.6 19.0 %all-to-all-done.2.p_ref = bf16[8,64,1024]{2,1,0:T(8,128)(2,1)S(1)} async-done(((bf16[8,64,1024]{2,1,0:T(8,128)(2,1)}), bf16[8,64,1024]{2,1,0:T(8,128)(2,1)S(1)}, u32[]{:S(2)}, u32[]{:S(2)}) %all-to-all-start.2) | async-done | bytes 1048608 | tf_op jit(solution)/shard_map/all_to_all | solution.py:373
  383.9 4.3 %all-to-all-done.3 = bf16[4,16,1024]{2,1,0:T(8,128)(2,1)S(1)} async-done(((bf16[4,16,1024]{2,1,0:T(8,128)(2,1)}), bf16[4,16,1024]{2,1,0:T(8,128)(2,1)S(1)}, u32[]{:S(2)}, u32[]{:S(2)}) %all-to-all-start.3) | async-done | bytes 131104 | tf_op jit(solution)/shard_map/all_to_all | solution.py:382
  (102 shorter events, 66.9 us)
Async XLA Ops:
  7.2 41.2 %all-gather.3.cloned.1.call-start = ((), (), s32[]{:S(2)}) async-start(), calls=%async_computation.4 | async-start | bytes 1216512 | tf_op jit(solution)/shard_map/all_gather | solution.py:326
  10.9 96.7 %all-gather.5.cloned.1.call-start = ((), (), s32[]{:S(2)}) async-start(), calls=%async_computation.5 | async-start | bytes 9732096 | tf_op jit(solution)/shard_map/all_gather | solution.py:327
  48.3 299.6 %collective-permute-start.15 = (bf16[1,2,4096,256]{3,2,1,0:T(8,128)(2,1)}, bf16[1,2,4096,256]{3,2,1,0:T(8,128)(2,1)}, u32[]{:S(2)}, u32[]{:S(2)}) collective-permute-start(bf16[1,2,4096,256]{3,2,1,0:T(8,128)(2,1)} %param.22), channel_id=1, source_target_pairs={{0,128},{4,132},{8,136},{12,140},{16,144},{20,148},{24,152},{28,15... | collective-permute-start | bytes 12582920 | tf_op jit(solution)/shard_map/ppermute | solution.py:282
  114.9 26.3 %collective-permute-start.10 = (bf16[128,4096]{1,0:T(8,128)(2,1)}, bf16[128,4096]{1,0:T(8,128)(2,1)S(1)}, u32[]{:S(2)}, u32[]{:S(2)}) collective-permute-start(bf16[128,4096]{1,0:T(8,128)(2,1)} %get-tuple-element.17.refs_0_), channel_id=1, source_target_pairs={{0,2},{1,3},{2,0},{3,1},{4,6},{5,7},{6,4},{7,5},{8,10},{9,11},{10,... | collective-permute-start | bytes 3145736 | tf_op jit(solution)/shard_map/ppermute | solution.py:266
  117.6 46.1 %collective-permute-start.11 = (bf16[128,4096]{1,0:T(8,128)(2,1)}, bf16[128,4096]{1,0:T(8,128)(2,1)S(1)}, u32[]{:S(2)}, u32[]{:S(2)}) collective-permute-start(bf16[128,4096]{1,0:T(8,128)(2,1)} %get-tuple-element.17.refs_0_), channel_id=1, source_target_pairs={{0,3},{1,0},{2,1},{3,2},{4,7},{5,4},{6,5},{7,6},{8,11},{9,8},{10,9... | collective-permute-start | bytes 3145736 | tf_op jit(solution)/shard_map/ppermute | solution.py:266
  118.5 57.0 %collective-permute-start.9 = (bf16[128,4096]{1,0:T(8,128)(2,1)}, bf16[128,4096]{1,0:T(8,128)(2,1)}, u32[]{:S(2)}, u32[]{:S(2)}) collective-permute-start(bf16[128,4096]{1,0:T(8,128)(2,1)} %get-tuple-element.17.refs_0_), channel_id=1, source_target_pairs={{0,1},{1,2},{2,3},{3,0},{4,5},{5,6},{6,7},{7,4},{8,9},{9,10},{10,1... | collective-permute-start | bytes 3145736 | tf_op jit(solution)/shard_map/ppermute | solution.py:266
  127.7 54.7 %collective-permute-start.6 = (bf16[256,1024]{1,0:T(8,128)(2,1)}, bf16[256,1024]{1,0:T(8,128)(2,1)S(1)}, u32[]{:S(2)}, u32[]{:S(2)}) collective-permute-start(bf16[256,1024]{1,0:T(8,128)(2,1)} %get-tuple-element.28), channel_id=1, source_target_pairs={{0,1},{1,2},{2,3},{3,0},{4,5},{5,6},{6,7},{7,4},{8,9},{9,10},{10,1... | collective-permute-start | bytes 1572872 | tf_op jit(solution)/shard_map/ppermute | solution.py:266
  141.2 44.9 %collective-permute-start.7 = (bf16[256,1024]{1,0:T(8,128)(2,1)}, bf16[256,1024]{1,0:T(8,128)(2,1)S(1)}, u32[]{:S(2)}, u32[]{:S(2)}) collective-permute-start(bf16[256,1024]{1,0:T(8,128)(2,1)} %get-tuple-element.27), channel_id=1, source_target_pairs={{0,2},{1,3},{2,0},{3,1},{4,6},{5,7},{6,4},{7,5},{8,10},{9,11},{10,... | collective-permute-start | bytes 1572872 | tf_op jit(solution)/shard_map/ppermute | solution.py:266
  163.7 22.5 %collective-permute-start.8 = (bf16[256,1024]{1,0:T(8,128)(2,1)}, bf16[256,1024]{1,0:T(8,128)(2,1)}, u32[]{:S(2)}, u32[]{:S(2)}) collective-permute-start(bf16[256,1024]{1,0:T(8,128)(2,1)} %get-tuple-element.26), channel_id=1, source_target_pairs={{0,3},{1,0},{2,1},{3,2},{4,7},{5,4},{6,5},{7,6},{8,11},{9,8},{10,9... | collective-permute-start | bytes 1572872 | tf_op jit(solution)/shard_map/ppermute | solution.py:266
  182.4 9.7 %collective-permute-start.12 = (bf16[512,256]{1,0:T(8,128)(2,1)}, bf16[512,256]{1,0:T(8,128)(2,1)S(1)}, u32[]{:S(2)}, u32[]{:S(2)}) collective-permute-start(bf16[512,256]{1,0:T(8,128)(2,1)} %gate_up.3.refs_0_), channel_id=1, source_target_pairs={{0,1},{1,2},{2,3},{3,0},{4,5},{5,6},{6,7},{7,4},{8,9},{9,10},{10,1... | collective-permute-start | bytes 786440 | tf_op jit(solution)/shard_map/ppermute | solution.py:266
  182.5 15.0 %collective-permute-start.13 = (bf16[512,256]{1,0:T(8,128)(2,1)}, bf16[512,256]{1,0:T(8,128)(2,1)S(1)}, u32[]{:S(2)}, u32[]{:S(2)}) collective-permute-start(bf16[512,256]{1,0:T(8,128)(2,1)} %gate_up.3.refs_0_), channel_id=1, source_target_pairs={{0,2},{1,3},{2,0},{3,1},{4,6},{5,7},{6,4},{7,5},{8,10},{9,11},{10,... | collective-permute-start | bytes 786440 | tf_op jit(solution)/shard_map/ppermute | solution.py:266
  186.1 12.1 %collective-permute-start.14 = (bf16[512,256]{1,0:T(8,128)(2,1)}, bf16[512,256]{1,0:T(8,128)(2,1)S(1)}, u32[]{:S(2)}, u32[]{:S(2)}) collective-permute-start(bf16[512,256]{1,0:T(8,128)(2,1)} %gate_up.3.refs_0_), channel_id=1, source_target_pairs={{0,3},{1,0},{2,1},{3,2},{4,7},{5,4},{6,5},{7,6},{8,11},{9,8},{10,9... | collective-permute-start | bytes 786440 | tf_op jit(solution)/shard_map/ppermute | solution.py:266
  186.2 34.0 %collective-permute-start = (bf16[128,4096]{1,0:T(8,128)(2,1)}, bf16[128,4096]{1,0:T(8,128)(2,1)}, u32[]{:S(2)}, u32[]{:S(2)}) collective-permute-start(bf16[128,4096]{1,0:T(8,128)(2,1)} %get-tuple-element.16.refs_0_), channel_id=1, source_target_pairs={{0,1},{1,2},{2,3},{3,0},{4,5},{5,6},{6,7},{7,4},{8,9},{9,10},{10,1... | collective-permute-start | bytes 3145736 | tf_op jit(solution)/shard_map/ppermute | solution.py:266
  192.2 50.2 %collective-permute-start.1 = (bf16[128,4096]{1,0:T(8,128)(2,1)}, bf16[128,4096]{1,0:T(8,128)(2,1)}, u32[]{:S(2)}, u32[]{:S(2)}) collective-permute-start(bf16[128,4096]{1,0:T(8,128)(2,1)} %get-tuple-element.16.refs_0_), channel_id=1, source_target_pairs={{0,2},{1,3},{2,0},{3,1},{4,6},{5,7},{6,4},{7,5},{8,10},{9,11},{10,... | collective-permute-start | bytes 3145736 | tf_op jit(solution)/shard_map/ppermute | solution.py:266
  197.4 45.0 %collective-permute-start.2 = (bf16[128,4096]{1,0:T(8,128)(2,1)}, bf16[128,4096]{1,0:T(8,128)(2,1)}, u32[]{:S(2)}, u32[]{:S(2)}) collective-permute-start(bf16[128,4096]{1,0:T(8,128)(2,1)} %get-tuple-element.16.refs_0_), channel_id=1, source_target_pairs={{0,3},{1,0},{2,1},{3,2},{4,7},{5,4},{6,5},{7,6},{8,11},{9,8},{10,9... | collective-permute-start | bytes 3145736 | tf_op jit(solution)/shard_map/ppermute | solution.py:266
  199.0 149.0 %collective-permute-start.17 = (bf16[1,256,4096]{2,1,0:T(8,128)(2,1)S(1)}, bf16[1,256,4096]{2,1,0:T(8,128)(2,1)}, u32[]{:S(2)}, u32[]{:S(2)}) collective-permute-start(bf16[1,256,4096]{2,1,0:T(8,128)(2,1)S(1)} %copy-done.1), channel_id=1, source_target_pairs={{0,128},{4,132},{8,136},{12,140},{16,144},{20,148},{24,152},{28,15... | collective-permute-start | bytes 6291464 | tf_op jit(solution)/shard_map/ppermute | solution.py:282
  209.3 61.1 %all-to-all-start.1 = ((bf16[8,8,8,1024]{3,2,1,0:T(8,128)(2,1)}), bf16[8,8,8,1024]{3,2,1,0:T(8,128)(2,1)S(1)}, u32[]{:S(2)}, u32[]{:S(2)}) async-start(bf16[8,8,8,1024]{3,2,1,0:T(8,128)(2,1)} %bitcast.37), calls=%async_computation.1 | async-start | bytes 2097152 | tf_op jit(solution)/shard_map/all_to_all | solution.py:362
  249.2 9.1 %collective-permute-start.3 = (bf16[512,256]{1,0:T(8,128)(2,1)}, bf16[512,256]{1,0:T(8,128)(2,1)S(1)}, u32[]{:S(2)}, u32[]{:S(2)}) collective-permute-start(bf16[512,256]{1,0:T(8,128)(2,1)} %gate_up.2.refs_0_), channel_id=1, source_target_pairs={{0,1},{1,2},{2,3},{3,0},{4,5},{5,6},{6,7},{7,4},{8,9},{9,10},{10,1... | collective-permute-start | bytes 786440 | tf_op jit(solution)/shard_map/ppermute | solution.py:266
  251.0 14.5 %collective-permute-start.4 = (bf16[512,256]{1,0:T(8,128)(2,1)}, bf16[512,256]{1,0:T(8,128)(2,1)}, u32[]{:S(2)}, u32[]{:S(2)}) collective-permute-start(bf16[512,256]{1,0:T(8,128)(2,1)} %gate_up.2.refs_0_), channel_id=1, source_target_pairs={{0,2},{1,3},{2,0},{3,1},{4,6},{5,7},{6,4},{7,5},{8,10},{9,11},{10,... | collective-permute-start | bytes 786440 | tf_op jit(solution)/shard_map/ppermute | solution.py:266
  253.7 11.8 %collective-permute-start.5 = (bf16[512,256]{1,0:T(8,128)(2,1)}, bf16[512,256]{1,0:T(8,128)(2,1)}, u32[]{:S(2)}, u32[]{:S(2)}) collective-permute-start(bf16[512,256]{1,0:T(8,128)(2,1)} %gate_up.2.refs_0_), channel_id=1, source_target_pairs={{0,3},{1,0},{2,1},{3,2},{4,7},{5,4},{6,5},{7,6},{8,11},{9,8},{10,9... | collective-permute-start | bytes 786440 | tf_op jit(solution)/shard_map/ppermute | solution.py:266
  270.4 74.3 %all-to-all-start = ((bf16[8,8,8,1024]{3,2,1,0:T(8,128)(2,1)}), bf16[8,8,8,1024]{3,2,1,0:T(8,128)(2,1)}, u32[]{:S(2)}, u32[]{:S(2)}) async-start(bf16[8,8,8,1024]{3,2,1,0:T(8,128)(2,1)} %bitcast.36), calls=%async_computation | async-start | bytes 2097152 | tf_op jit(solution)/shard_map/all_to_all | solution.py:362
  276.0 71.9 %collective-permute-start.16 = (bf16[1,2,32,2]{2,3,1,0:T(2,128)(2,1)S(1)}, bf16[1,2,32,2]{2,3,1,0:T(2,128)(2,1)S(1)}, u32[]{:S(2)}, u32[]{:S(2)}) collective-permute-start(bf16[1,2,32,2]{2,3,1,0:T(2,128)(2,1)S(1)} %copy-done.14), channel_id=1, source_target_pairs={{0,128},{4,132},{8,136},{12,140},{16,144},{20,148},{24,152},{28,15... | collective-permute-start | bytes 776 | tf_op jit(solution)/shard_map/ppermute | solution.py:282
  281.5 66.4 %collective-permute-start.18 = (bf16[1,2,32]{2,1,0:T(2,128)(2,1)S(1)}, bf16[1,2,32]{2,1,0:T(2,128)(2,1)S(1)}, u32[]{:S(2)}, u32[]{:S(2)}) collective-permute-start(bf16[1,2,32]{2,1,0:T(2,128)(2,1)S(1)} %copy-done.15), channel_id=1, source_target_pairs={{0,128},{4,132},{8,136},{12,140},{16,144},{20,148},{24,152},{28,15... | collective-permute-start | bytes 392 | tf_op jit(solution)/shard_map/ppermute | solution.py:282
  348.0 28.7 %all-to-all-start.2 = ((bf16[8,64,1024]{2,1,0:T(8,128)(2,1)}), bf16[8,64,1024]{2,1,0:T(8,128)(2,1)S(1)}, u32[]{:S(2)}, u32[]{:S(2)}) async-start(bf16[8,64,1024]{2,1,0:T(8,128)(2,1)} %bitcast.35), calls=%async_computation.2 | async-start | bytes 2097152 | tf_op jit(solution)/shard_map/all_to_all | solution.py:373
  (19 other events, 319.5 us)
Sparse Core Ops, SparseCore 0:
  11.0 37.2 all-gather.2
  50.1 57.3 all-gather.4

commit v2 on v1

v2 whole, which is shorter than its diff:
```python
import jax
import jax.numpy as jnp
from jax import lax
from jax.experimental import pallas as pl
from jax.experimental.pallas import tpu as pltpu
from jax.sharding import PartitionSpec as P


BF16 = jnp.bfloat16
F32 = jnp.float32
I32 = jnp.int32
TOK = 8
CAP = 2
LANES = 128
PLANE = 8
VMEM = pltpu.VMEM
SMEM = pltpu.SMEM


def iota(shape, dim):
    return lax.broadcasted_iota(I32, shape, dim)


def vspec():
    return pl.BlockSpec(memory_space=VMEM)


def sspec():
    return pl.BlockSpec(memory_space=SMEM)


def gate_up_dequant(values, scale_rows):
    _, features, width = values.shape
    rows = features // 4
    blocks = rows // LANES

    def kernel(v_ref, s_ref, o_ref):
        wide = v_ref[0].astype(F32).reshape(blocks, LANES, width)
        o_ref[0] = (wide * s_ref[0][:, None, :]).reshape(rows, width).astype(BF16)

    return pl.pallas_call(
        kernel,
        grid=(2, 4),
        in_specs=[
            pl.BlockSpec((1, rows, width), lambda g, i: (g, i, 0)),
            pl.BlockSpec((1, blocks, width), lambda g, i: (g, i, 0)),
        ],
        out_specs=pl.BlockSpec((1, rows, width), lambda g, i: (g, i, 0)),
        out_shape=jax.ShapeDtypeStruct(values.shape, BF16),
        name="gate_up_dequant",
    )(values, scale_rows)


def down_dequant(values, scale_rows, order):
    height, features = values.shape
    copies = order.shape[0]
    width = features // copies
    blocks = scale_rows.shape[0]

    def kernel(order_ref, v_ref, s_ref, o_ref):
        wide = v_ref[...].astype(F32).reshape(blocks, height // blocks, width)
        o_ref[0] = (wide * s_ref[...][:, None, :]).reshape(height, width).astype(BF16)

    return pl.pallas_call(
        kernel,
        grid_spec=pltpu.PrefetchScalarGridSpec(
            num_scalar_prefetch=1,
            grid=(copies,),
            in_specs=[
                pl.BlockSpec((height, width), lambda k, o: (0, o[k])),
                pl.BlockSpec((blocks, width), lambda k, o: (0, o[k])),
            ],
            out_specs=pl.BlockSpec((1, height, width), lambda k, o: (k, 0, 0)),
        ),
        out_shape=jax.ShapeDtypeStruct((copies, height, width), BF16),
        name="down_dequant",
    )(order, values, scale_rows)


def norm_and_pack(hidden, routes, mixing, gain, levels):
    rows, features = hidden[0].shape
    top = routes[0].shape[1]

    def kernel(h0, h1, r0, r1, m0, m1, g_ref, o_ref):
        lane, entry = iota((top, LANES), 1), iota((top, LANES), 0)
        for at, h_ref, r_ref, m_ref in ((0, h0, r0, m0), (rows, h1, r1, m1)):
            wide = h_ref[...].astype(F32)
            inverse = lax.rsqrt(jnp.mean(wide * wide, axis=-1, keepdims=True) + 1e-06)
            normed = (wide * inverse * g_ref[...]).astype(BF16)
            high = m_ref[...].astype(BF16)
            rest = m_ref[...] - high.astype(F32)
            middle = rest.astype(BF16)
            low = (rest - middle.astype(F32)).astype(BF16)
            picks = jnp.zeros((rows, LANES), F32)
            for part, values in enumerate((r_ref[...].astype(F32).astype(BF16), high, middle, low)):
                put = jnp.where(lane == entry + part * top, 1.0, 0.0).astype(BF16)
                picks = picks + jnp.dot(values, put, preferred_element_type=F32)
            picks = picks.astype(BF16)
            for level in range(levels):
                o_ref[level, at : at + rows, :features] = normed
                o_ref[level, at : at + rows, features:] = picks

    return pl.pallas_call(
        kernel,
        in_specs=[vspec()] * 7,
        out_specs=vspec(),
        out_shape=jax.ShapeDtypeStruct((levels, 2 * rows, features + LANES), BF16),
        name="norm_and_pack",
    )(*hidden, *routes, *mixing, gain)


def select_rows(column, plane_experts, top):
    rows, packed = column.shape
    features = packed - LANES
    groups = rows // TOK
    kept = PLANE * groups * CAP

    def kernel(e_ref, c_ref, o_ref):
        at = e_ref[...].astype(F32)
        ids = c_ref[:, features:].astype(F32)
        hit = jnp.zeros((rows, kept), F32)
        for k in range(top):
            hit = hit + jnp.where(ids[:, k : k + 1] == at, 1.0, 0.0)
        r, q = iota((rows, rows), 0), iota((rows, rows), 1)
        before = jnp.where(((r >> 3) == (q >> 3)) & (q < r), 1.0, 0.0).astype(BF16)
        rank = jnp.dot(before, hit.astype(BF16), preferred_element_type=F32)
        row, col = iota((rows, kept), 0), iota((rows, kept), 1)
        own_group = (row >> 3) == ((col >> 1) & (groups - 1))
        chosen = own_group & (rank == (col & 1).astype(F32)) & (hit > 0.5)
        picking = jnp.where(chosen, 1.0, 0.0).astype(BF16)
        for start in range(0, features, 1024):
            o_ref[:, start : start + 1024] = lax.dot_general(
                picking,
                c_ref[:, start : start + 1024],
                (((0,), (0,)), ((), ())),
                preferred_element_type=F32,
            ).astype(BF16)

    return pl.pallas_call(
        kernel,
        in_specs=[vspec(), vspec()],
        out_specs=vspec(),
        out_shape=jax.ShapeDtypeStruct((kept, features), BF16),
        name="select_rows",
    )(jnp.repeat(plane_experts, groups * CAP).reshape(1, kept), column)


def gate_up(pieces, weights, columns):
    copies = len(pieces)
    rows, features = pieces[0].shape
    width = weights.shape[2]

    def kernel(c_ref, *refs):
        x_refs, w_ref, o_ref, x_all = refs[:copies], refs[copies], refs[copies + 1], refs[copies + 2]
        for k in range(copies):
            start = pl.multiple_of(c_ref[k] * rows, rows)
            x_all[pl.ds(start, rows), :] = x_refs[k][...]
        gate = jnp.dot(x_all[...], w_ref[0], preferred_element_type=F32)
        up = jnp.dot(x_all[...], w_ref[1], preferred_element_type=F32)
        o_ref[...] = (gate / (1.0 + jnp.exp(-gate)) * up).astype(BF16)

    return pl.pallas_call(
        kernel,
        in_specs=[sspec()] + [vspec()] * (copies + 1),
        out_specs=vspec(),
        out_shape=jax.ShapeDtypeStruct((copies * rows, width), BF16),
        scratch_shapes=[pltpu.VMEM((copies * rows, features), BF16)],
        name="gate_up",
    )(columns, *pieces, weights)


def down(inner, weights):
    copies = len(inner)
    rows, width_in = inner[0].shape
    width = weights[0].shape[1]
    piece = rows // copies // PLANE
    group = piece * copies
    unit = 2 * CAP

    def kernel(*refs):
        i_refs, w_refs, o_ref, placed = (
            refs[:copies],
            refs[copies : 2 * copies],
            refs[2 * copies],
            refs[2 * copies + 1],
        )
        r, q = iota((group, group), 0), iota((group, group), 1)
        copy, level = (r >> 2) & (copies - 1), r >> 4
        source = copy * piece + level * unit + (r & 3)
        order = jnp.where(q == source, 1.0, 0.0).astype(BF16)
        total = jnp.zeros((rows, width), F32)
        for i_ref, w_ref in zip(i_refs, w_refs):
            for member in range(PLANE):
                parts = [
                    i_ref[(c * PLANE + member) * piece : (c * PLANE + member + 1) * piece, :]
                    for c in range(copies)
                ]
                placed[member * group : (member + 1) * group, :] = jnp.dot(
                    order, jnp.concatenate(parts, axis=0), preferred_element_type=F32
                ).astype(BF16)
            total = total + jnp.dot(placed[...], w_ref[...], preferred_element_type=F32)
        o_ref[...] = total.astype(BF16)

    return pl.pallas_call(
        kernel,
        in_specs=[vspec()] * (2 * copies),
        out_specs=vspec(),
        out_shape=jax.ShapeDtypeStruct((rows, width), BF16),
        scratch_shapes=[pltpu.VMEM((rows, width_in), BF16)],
        name="down",
    )(*inner, *weights)


def mixing_tables(picks, plane_experts, copies, top):
    tokens = picks.shape[0]
    places = PLANE * copies * 2 * CAP
    column = tokens // copies

    def kernel(p_ref, e_ref, high_ref, low_ref):
        at = e_ref[...].astype(F32)
        packed = p_ref[...].astype(F32)
        hit = jnp.zeros((tokens, places), F32)
        weight = jnp.zeros((tokens, places), F32)
        for k in range(top):
            same = packed[:, k : k + 1] == at
            mix = (
                packed[:, top + k : top + k + 1]
                + packed[:, 2 * top + k : 2 * top + k + 1]
                + packed[:, 3 * top + k : 3 * top + k + 1]
            )
            hit = hit + jnp.where(same, 1.0, 0.0)
            weight = weight + jnp.where(same, mix, 0.0)
        r, q = iota((column, column), 0), iota((column, column), 1)
        before = jnp.where(((r >> 3) == (q >> 3)) & (q < r), 1.0, 0.0).astype(BF16)
        row, col = iota((column, places), 0), iota((column, places), 1)
        for copy in range(copies):
            rows = slice(copy * column, (copy + 1) * column)
            rank = jnp.dot(before, hit[rows].astype(BF16), preferred_element_type=F32)
            here = (
                (((col >> 2) & (copies - 1)) == copy)
                & (((row >> 3) & 1) == ((col >> 1) & 1))
                & (rank == (col & 1).astype(F32))
            )
            kept = jnp.where(here, weight[rows], 0.0)
            high = kept.astype(BF16)
            high_ref[rows, :] = high
            low_ref[rows, :] = (kept - high.astype(F32)).astype(BF16)

    shape = jax.ShapeDtypeStruct((tokens, places), BF16)
    return pl.pallas_call(
        kernel,
        in_specs=[vspec(), vspec()],
        out_specs=[vspec()] * 2,
        out_shape=[shape] * 2,
        name="mixing_tables",
    )(picks, jnp.repeat(plane_experts, copies * 2 * CAP).reshape(1, places))


def combine(returned, tables, copies):
    members, levels, rows, width = returned.shape
    tokens = copies * 2 * TOK
    column = levels * 2 * TOK

    def kernel(r_ref, h_ref, l_ref, o_ref):
        for level in range(levels):
            found = r_ref[:, level].reshape(members * rows, width)
            total = jnp.zeros((tokens, width), F32)
            for t_ref in (h_ref, l_ref):
                first = level * 2 * TOK
                table = jnp.concatenate(
                    [
                        t_ref[c * column + first : c * column + first + 2 * TOK, :]
                        for c in range(copies)
                    ],
                    axis=0,
                )
                total = total + jnp.dot(table, found, preferred_element_type=F32)
            o_ref[level] = total.astype(BF16)

    return pl.pallas_call(
        kernel,
        in_specs=[vspec()] * 3,
        out_specs=vspec(),
        out_shape=jax.ShapeDtypeStruct((levels, tokens, width), BF16),
        name="combine",
    )(returned, *tables)


def add_levels(parts):
    levels, rows, width = parts.shape

    def kernel(p_ref, o_ref):
        total = p_ref[0].astype(F32)
        for level in range(1, levels):
            total = total + p_ref[level].astype(F32)
        o_ref[...] = total.astype(BF16)

    return pl.pallas_call(
        kernel,
        in_specs=[vspec()],
        out_specs=vspec(),
        out_shape=jax.ShapeDtypeStruct((rows, width), BF16),
        name="add_levels",
    )(parts)


def shifted(block, shift):
    copies = lax.axis_size("replica")
    return lax.ppermute(block, "replica", [(i, (i + shift) % copies) for i in range(copies)])


def level_groups():
    experts = lax.axis_size("expert")
    return [list(range(member, experts, PLANE)) for member in range(PLANE)]


def plane_groups():
    experts = lax.axis_size("expert")
    return [list(range(at, at + PLANE)) for at in range(0, experts, PLANE)]


def swapped(block):
    experts = lax.axis_size("expert")
    half = experts // 2
    return lax.ppermute(block, "expert", [(i, (i + half) % experts) for i in range(experts)])


def layer(
    hidden_first,
    hidden_second,
    routes_first,
    routes_second,
    mixing_first,
    mixing_second,
    norm_gain,
    expert_owner,
    swap_flags,
    gate_up_values,
    gate_up_scales,
    down_values,
    down_scales,
):
    experts = lax.axis_size("expert")
    copies = lax.axis_size("replica")
    levels = experts // PLANE
    my_slot = lax.axis_index("expert")
    my_copy = lax.axis_index("replica")
    features = hidden_first.shape[1]
    width = features // copies
    top = routes_first.shape[1]
    slot_ids = jnp.arange(experts, dtype=I32)
    hops = jnp.arange(copies, dtype=I32)
    ahead = (my_copy + hops) % copies
    behind = (my_copy - hops + copies) % copies

    plane_slots = my_slot // PLANE * PLANE + jnp.arange(PLANE, dtype=I32)
    plane_experts = jnp.sum(
        jnp.where(expert_owner[:, None] == plane_slots[None, :], slot_ids[:, None], 0), axis=0
    )

    packs = norm_and_pack(
        (hidden_first, hidden_second),
        (routes_first, routes_second),
        (mixing_first, mixing_second),
        norm_gain.reshape(1, features),
        levels,
    )
    column = lax.all_to_all(
        packs, "expert", 0, 0, tiled=True, axis_index_groups=level_groups()
    )
    column = column.reshape(levels * 2 * TOK, features + LANES)

    flagged = jnp.sum(jnp.where(slot_ids == my_slot, swap_flags, 0)) == 1
    cut = down_values.shape[1] * 13 // 16
    early_piece, late_piece = down_values[0, :cut], down_values[0, cut:]
    gate_up_in = swapped(gate_up_values)
    scales = (gate_up_scales, down_scales)
    tail = jnp.concatenate([scale.reshape(-1) for scale in scales])
    tail = jnp.pad(tail, (0, TOK * features - tail.size)).reshape(TOK, features)
    early_in = swapped(jnp.concatenate([early_piece, tail]))

    own_rows = select_rows(column, plane_experts, top)
    own_rows = lax.all_to_all(
        own_rows.reshape(PLANE, -1, features),
        "expert",
        0,
        0,
        tiled=True,
        axis_index_groups=plane_groups(),
    ).reshape(own_rows.shape)

    picks = lax.all_gather(column[:, features:], "replica", axis=0, tiled=True)
    tables = mixing_tables(picks, plane_experts, copies, top)
    gate_up_rows = jnp.repeat(gate_up_scales[0].astype(F32), LANES, axis=-1)
    down_rows = jnp.repeat(down_scales[0].astype(F32), LANES, axis=-1)
    down_sent = down_dequant(down_values[0], down_rows, ahead)
    down_weights = [down_sent[0]] + [shifted(down_sent[k], k) for k in range(1, copies)]
    gate_up_weights = gate_up_dequant(gate_up_values[0], gate_up_rows)

    pieces = [own_rows] + [shifted(own_rows, k) for k in range(1, copies)]

    inner = gate_up(pieces, gate_up_weights, behind)
    inners = [inner] + [shifted(inner, k) for k in range(1, copies)]
    results = down(inners, down_weights)
    returned = lax.all_to_all(
        results.reshape(PLANE, levels, -1, width),
        "expert",
        0,
        0,
        tiled=True,
        axis_index_groups=plane_groups(),
    )
    mixed = combine(returned, tables, copies)
    parts = lax.all_to_all(
        mixed, "expert", 0, 0, tiled=True, axis_index_groups=level_groups()
    )
    late_in = swapped(late_piece)
    summed = add_levels(parts).reshape(copies, 2 * TOK, width)
    spread = lax.all_to_all(summed, "replica", split_axis=0, concat_axis=0, tiled=True)
    outputs = tuple(
        spread[:, step * TOK : (step + 1) * TOK].transpose(1, 0, 2).reshape(TOK, features)
        for step in range(2)
    )

    gate_up_in, early_in, _ = lax.optimization_barrier((gate_up_in, early_in, mixed))
    tail_in = early_in[cut]
    count = gate_up_scales.size
    scales_in = (
        tail_in[:count].reshape(gate_up_scales.shape),
        tail_in[count : count + down_scales.size].reshape(down_scales.shape),
    )
    gate_up_moved = jnp.where(flagged, gate_up_in, gate_up_values)
    gate_up_scales_moved = jnp.where(flagged, scales_in[0], gate_up_scales)
    down_scales_moved = jnp.where(flagged, scales_in[1], down_scales)
    down_in = jnp.concatenate([early_in[:cut], late_in])[None]
    down_moved = jnp.where(flagged, down_in, down_values)
    return outputs + (gate_up_moved, gate_up_scales_moved, down_moved, down_scales_moved)


def solution(mesh):
    tokens = P(("expert", "replica"), None)
    weights = (
        P("expert", None, None, "replica"),
        P("expert", None, None, "replica"),
        P("expert", "replica", None),
        P("expert", "replica", None),
    )
    return jax.shard_map(
        layer,
        mesh=mesh,
        in_specs=(tokens,) * 6 + (P(),) * 3 + weights,
        out_specs=(tokens,) * 2 + weights,
        check_vma=False,
    )
```

time: 402 us -> 402 us (level)
  waiting for transfers between devices: 195 us -> 236 us
  starting transfers between devices: 56.2 us -> 40.2 us
  blocking collectives: 58 us -> 42.1 us
  between operations: 14.8 us -> 1.41 us
  local copies, waits for them, and re-layouts: 10.4 us -> 20.4 us
  Pallas kernels: 52 us -> 42.4 us
  other arithmetic: 9 us -> 14.1 us
    ppermute x4 -> x3, waiting for transfers between devices: 0.01 us -> 94 us  [swapped(): lax.ppermute(block, 'expert', [(i, (i + half) % experts) for i in range(e...]
    all_gather x2 -> x0, waiting for transfers between devices: 92.1 us -> none  [the longest x1 54.7 us: layer(): lax.all_gather(column, 'expert', axis=0, tiled=True, axis_index_groups=pl...]
    all_gather x2 -> x1, blocking collectives: 58 us -> 10.7 us  [layer(): picks = lax.all_gather(column[:, features:], 'replica', axis=0, tiled=True)]
    all_to_all x0 -> x1, blocking collectives: none -> 31.4 us  [layer(): lax.all_to_all(own_rows.reshape(PLANE, -1, features), 'expert', 0, 0, til...]
    all_to_all x3, waiting for transfers between devices: 19 us -> 42.4 us  [the longest x1 29 us: layer(): lax.all_to_all(packs, 'expert', 0, 0, tiled=True, axis_index_groups=level...]
    ppermute x15 -> x9, waiting for transfers between devices: 79.8 us -> 96.5 us  [shifted(): lax.ppermute(block, 'replica', [(i, (i + shift) % copies) for i in range(...]
    ppermute x15 -> x9, starting transfers between devices: 22.5 us -> 11.8 us  [shifted(): lax.ppermute(block, 'replica', [(i, (i + shift) % copies) for i in range(...]
    ppermute x4 -> x3, starting transfers between devices: 14.2 us -> 5.65 us  [swapped(): lax.ppermute(block, 'expert', [(i, (i + half) % experts) for i in range(e...]
  transfers between devices with their start and end apart: 25 -> 16, of which waited for: 15 -> 11; matrix products, arithmetic and copies ran while one was open for 3% -> 8% of each run, Pallas kernels for 12% -> 9%
where the time goes in v2:
time: 402 us; the launch traced here: 397 us
  waiting for transfers between devices  236 us (59%)
  Pallas kernels  42.4 us (11%)
  blocking collectives  42.1 us (10%)
  starting transfers between devices  40.2 us (10%)
  local copies, waits for them, and re-layouts  20.4 us (5%)
  other arithmetic  14.1 us (4%)
    ppermute x9, waiting for transfers between devices, shifted(): lax.ppermute(block, 'replica', [(i, (i + shift) % copies) for i in range(...  96.5 us
    ppermute x3, waiting for transfers between devices, swapped(): lax.ppermute(block, 'expert', [(i, (i + half) % experts) for i in range(e...  94 us
    all_to_all x1, blocking collectives, layer(): lax.all_to_all(own_rows.reshape(PLANE, -1, features), 'expert', 0, 0, til...  31.4 us
    all_to_all x1, waiting for transfers between devices, layer(): lax.all_to_all(packs, 'expert', 0, 0, tiled=True, axis_index_groups=level...  29 us
    all_to_all x1, waiting for transfers between devices, layer(): lax.all_to_all(mixed, 'expert', 0, 0, tiled=True, axis_index_groups=level...  12.4 us
    ppermute x9, starting transfers between devices, shifted(): lax.ppermute(block, 'replica', [(i, (i + shift) % copies) for i in range(...  11.8 us
    all_gather x1, blocking collectives, layer(): picks = lax.all_gather(column[:, features:], 'replica', axis=0, tiled=True)  10.7 us
    pallas_call x1, Pallas kernels, gate_up(): pl.pallas_call(kernel, in_specs=[sspec()] + [vspec()] * (copies + 1), out...  10.6 us
  transfers between devices with their start and end apart: 16, of which 11 were waited for; matrix products, arithmetic and copies ran while one was open for 8% of the time, Pallas kernels for 9%

profile of v2, /device:TPU:1, one launch (start us, length us, event | category | flops | bytes accessed | tf_op | source)
XLA Modules:
  0.0 397.0 jit_solution(12439434959374263700)
XLA Ops:
  2.8 9.0 %all-to-all-start = ((bf16[8,16,4224]{2,1,0:T(8,128)(2,1)}), bf16[8,16,4224]{2,1,0:T(8,128)(2,1)S(1)}, u32[]{:S(2)}, u32[]{:S(2)}) async-start(bf16[8,16,4224]{2,1,0:T(8,128)(2,1)} %norm_and_pack.1), calls=%async_computation | async-start | bytes 2162688 | tf_op jit(solution)/shard_map/all_to_all | solution.py:368
  12.7 29.0 %all-to-all-done = bf16[8,16,4224]{2,1,0:T(8,128)(2,1)S(1)} async-done(((bf16[8,16,4224]{2,1,0:T(8,128)(2,1)}), bf16[8,16,4224]{2,1,0:T(8,128)(2,1)S(1)}, u32[]{:S(2)}, u32[]{:S(2)}) %all-to-all-start) | async-done | bytes 1081376 | tf_op jit(solution)/shard_map/all_to_all | solution.py:368
  42.6 3.6 select_rows.1
  46.3 31.4 %all_to_all.25 = bf16[8,32,4096]{2,1,0:T(8,128)(2,1)} all-to-all(bf16[8,32,4096]{2,1,0:T(8,128)(2,1)} %bitcast.45), channel_id=1, replica_groups={{0,4,8,12,16,20,24,28},{32,36,40,44,48,52,56,60},{64,68,72,76,80,84,88,..., dimensions={0} | all-to-all | bytes 4194304 | tf_op jit(solution)/shard_map/all_to_all | solution.py:383
  84.0 4.6 %down_dequant.1 = bf16[4,256,1024]{2,1,0:T(8,128)(2,1)} custom-call(s32[4]{0:T(128)} %and_select_fusion.order_ref, bf16[256,4096]{1,0:T(8,128)(2,1)} %bitcast.43, f32[2,4096]{1,0:T(2,128)} %bitcast.49), custom_call_target="tpu_custom_call" | custom-call | tf_op jit(solution)/shard_map/down_dequant/pallas_call | solution.py:64
  93.1 32.3 %collective-permute-done.refs_1_ = bf16[256,4096]{1,0:T(8,128)(2,1)S(1)} collective-permute-done((bf16[256,4096]{1,0:T(8,128)(2,1)}, bf16[256,4096]{1,0:T(8,128)(2,1)S(1)}, u32[]{:S(2)}, u32[]{:S(2)}) %collective-permute-start) | collective-permute-done | bytes 2097184 | tf_op jit(solution)/shard_map/ppermute | solution.py:309
  126.9 6.8 %gate_up_dequant.1.refs_4_ = bf16[2,4096,256]{2,1,0:T(8,128)(2,1)} custom-call(bf16[2,4096,256]{2,1,0:T(8,128)(2,1)} %bitcast.4.v_ref, f32[2,32,256]{2,1,0:T(8,128)} %reshape.74.s_ref), custom_call_target="tpu_custom_call" | custom-call | tf_op jit(solution)/shard_map/gate_up_dequant/pallas_call | solution.py:41
  134.3 37.0 %collective-permute-done.1.refs_2_ = bf16[256,4096]{1,0:T(8,128)(2,1)} collective-permute-done((bf16[256,4096]{1,0:T(8,128)(2,1)}, bf16[256,4096]{1,0:T(8,128)(2,1)}, u32[]{:S(2)}, u32[]{:S(2)}) %collective-permute-start.1) | collective-permute-done | bytes 2097184 | tf_op jit(solution)/shard_map/ppermute | solution.py:309
  172.4 10.6 %gate_up.1.refs_0_ = bf16[1024,256]{1,0:T(8,128)(2,1)} custom-call(s32[4]{0:T(128)} %and_select_fusion.1.c_ref, bf16[256,4096]{1,0:T(8,128)(2,1)} %bitcast.3.refs_0_, bf16[256,4096]{1,0:T(8,128)(2,1)} %copy-done.3, bf16[256,4096]{1,0:T(8,128)(2,1)} %collective-permute-done.1.refs_2_, bf16[256,4096]{1,0:T(8,128)(2,1)} %collective-permute-done.2.refs_3_, ...), custom_call_target="tpu_custom_call" | custom-call | tf_op jit(solution)/shard_map/gate_up/pallas_call | solution.py:162
  183.8 4.2 %collective-permute-start.4 = (bf16[1024,256]{1,0:T(8,128)(2,1)}, bf16[1024,256]{1,0:T(8,128)(2,1)}, u32[]{:S(2)}, u32[]{:S(2)}) collective-permute-start(bf16[1024,256]{1,0:T(8,128)(2,1)} %gate_up.1.refs_0_), channel_id=1, source_target_pairs={{0,2},{1,3},{2,0},{3,1},{4,6},{5,7},{6,4},{7,5},{8,10},{9,11},{10,... | collective-permute-start | bytes 1572872 | tf_op jit(solution)/shard_map/ppermute | solution.py:309
  188.0 5.8 %collective-permute-done.7.refs_6_ = bf16[256,1024]{1,0:T(8,128)(2,1)S(1)} collective-permute-done((bf16[256,1024]{1,0:T(8,128)(2,1)}, bf16[256,1024]{1,0:T(8,128)(2,1)S(1)}, u32[]{:S(2)}, u32[]{:S(2)}) %collective-permute-start.7) | collective-permute-done | bytes 524320 | tf_op jit(solution)/shard_map/ppermute | solution.py:309
  195.2 8.4 %collective-permute-done.3.refs_1_ = bf16[1024,256]{1,0:T(8,128)(2,1)} collective-permute-done((bf16[1024,256]{1,0:T(8,128)(2,1)}, bf16[1024,256]{1,0:T(8,128)(2,1)}, u32[]{:S(2)}, u32[]{:S(2)}) %collective-permute-start.3) | collective-permute-done | bytes 524320 | tf_op jit(solution)/shard_map/ppermute | solution.py:309
  203.6 12.0 %collective-permute-done.4.refs_2_ = bf16[1024,256]{1,0:T(8,128)(2,1)} collective-permute-done((bf16[1024,256]{1,0:T(8,128)(2,1)}, bf16[1024,256]{1,0:T(8,128)(2,1)}, u32[]{:S(2)}, u32[]{:S(2)}) %collective-permute-start.4) | collective-permute-done | bytes 524320 | tf_op jit(solution)/shard_map/ppermute | solution.py:309
  215.6 6.3 %down.1 = bf16[1024,1024]{1,0:T(8,128)(2,1)} custom-call(bf16[1024,256]{1,0:T(8,128)(2,1)} %gate_up.1.refs_0_, bf16[1024,256]{1,0:T(8,128)(2,1)} %collective-permute-done.3.refs_1_, bf16[1024,256]{1,0:T(8,128)(2,1)} %collective-permute-done.4.refs_2_, bf16[1024,256]{1,0:T(8,128)(2,1)} %collective-permute-done.5.refs_3_, ...), custom_call_target="tpu_custom_call" | custom-call | tf_op jit(solution)/shard_map/down/pallas_call | solution.py:204
  221.9 6.9 %all-to-all-start.2 = ((bf16[8,8,16,1024]{3,2,1,0:T(8,128)(2,1)}), bf16[8,8,16,1024]{3,2,1,0:T(8,128)(2,1)}, u32[]{:S(2)}, u32[]{:S(2)}) async-start(bf16[8,8,16,1024]{3,2,1,0:T(8,128)(2,1)} %bitcast.44), calls=%async_computation.2 | async-start | bytes 4194304 | tf_op jit(solution)/shard_map/all_to_all | solution.py:405
  232.7 5.1 %collective-permute-start.11 = (bf16[48,4096]{1,0:T(8,128)(2,1)}, bf16[48,4096]{1,0:T(8,128)(2,1)S(1)}, u32[]{:S(2)}, u32[]{:S(2)}) collective-permute-start(bf16[48,4096]{1,0:T(8,128)(2,1)} %slice_bitcast_fusion.5), channel_id=1, source_target_pairs={{0,128},{4,132},{8,136},{12,140},{16,144},{20,148},{24,152},{28,15... | collective-permute-start | bytes 1179656 | tf_op jit(solution)/shard_map/ppermute | solution.py:325
  240.5 10.7 %all_gather.3.p_ref = bf16[512,128]{1,0:T(8,128)(2,1)} all-gather(bf16[128,128]{1,0:T(8,128)(2,1)S(1)} %slice.57), channel_id=1, replica_groups=mesh['expert'=64,'replica'=4] {'replica'}, dimensions={0}, use_global_device_ids=true | all-gather | bytes 163840 | tf_op jit(solution)/shard_map/all_gather | solution.py:392
  255.1 3.4 combine.1
  258.5 94.0 %collective-permute-done.10 = bf16[216,4096]{1,0:T(8,128)(2,1)} collective-permute-done((bf16[216,4096]{1,0:T(8,128)(2,1)}, bf16[216,4096]{1,0:T(8,128)(2,1)}, u32[]{:S(2)}, u32[]{:S(2)}) %collective-permute-start.10) | collective-permute-done | bytes 1769504 | tf_op jit(solution)/shard_map/ppermute | solution.py:325
  356.6 3.6 all-to-all-start.3
  364.6 3.6 fusion
  368.2 4.7 %broadcast_select_fusion = bf16[1,2,4096,256]{3,2,1,0:T(8,128)(2,1)} fusion(bf16[1,2,4096,256]{3,2,1,0:T(8,128)(2,1)} %collective-permute-done.9, bf16[1,2,4096,256]{3,2,1,0:T(8,128)(2,1)} %param.22, pred[]{:T(512)S(6)} %eq.30), kind=kLoop, calls=%fused_computation | loop fusion | flops 2097152 | bytes 12582913 | tf_op jit(solution)/shard_map/jit(_where)/select_n | solution.py:432
  372.9 12.4 %all-to-all-done.3.p_ref = bf16[8,64,1024]{2,1,0:T(8,128)(2,1)S(1)} async-done(((bf16[8,64,1024]{2,1,0:T(8,128)(2,1)}), bf16[8,64,1024]{2,1,0:T(8,128)(2,1)S(1)}, u32[]{:S(2)}, u32[]{:S(2)}) %all-to-all-start.3) | async-done | bytes 1048608 | tf_op jit(solution)/shard_map/all_to_all | solution.py:414
  392.8 3.6 all-to-all-done.4
  (86 shorter events, 46.9 us)
Async XLA Ops:
  2.8 38.9 %all-to-all-start = ((bf16[8,16,4224]{2,1,0:T(8,128)(2,1)}), bf16[8,16,4224]{2,1,0:T(8,128)(2,1)S(1)}, u32[]{:S(2)}, u32[]{:S(2)}) async-start(bf16[8,16,4224]{2,1,0:T(8,128)(2,1)} %norm_and_pack.1), calls=%async_computation | async-start | bytes 2162688 | tf_op jit(solution)/shard_map/all_to_all | solution.py:368
  12.0 65.7 %copy-start.8 = (s32[8]{0:T(128)}, s32[8]{0:T(128)S(1)}, u32[]{:S(2)}) copy-start(s32[8]{0:T(128)S(1)} %select_reduce_fusion) | copy-start | bytes 100
  46.3 36.5 %copy-start.10 = (bf16[1,2,32]{2,1,0:T(2,128)(2,1)S(1)}, bf16[1,2,32]{2,1,0:T(2,128)(2,1)}, u32[]{:S(2)}) copy-start(bf16[1,2,32]{2,1,0:T(2,128)(2,1)} %param.25) | copy-start | bytes 388
  77.6 47.7 %collective-permute-start = (bf16[256,4096]{1,0:T(8,128)(2,1)}, bf16[256,4096]{1,0:T(8,128)(2,1)S(1)}, u32[]{:S(2)}, u32[]{:S(2)}) collective-permute-start(bf16[256,4096]{1,0:T(8,128)(2,1)} %bitcast.3.refs_0_), channel_id=1, source_target_pairs={{0,1},{1,2},{2,3},{3,0},{4,5},{5,6},{6,7},{7,4},{8,9},{9,10},{10,1... | collective-permute-start | bytes 6291464 | tf_op jit(solution)/shard_map/ppermute | solution.py:309
  78.9 92.4 %collective-permute-start.1 = (bf16[256,4096]{1,0:T(8,128)(2,1)}, bf16[256,4096]{1,0:T(8,128)(2,1)}, u32[]{:S(2)}, u32[]{:S(2)}) collective-permute-start(bf16[256,4096]{1,0:T(8,128)(2,1)} %bitcast.3.refs_0_), channel_id=1, source_target_pairs={{0,2},{1,3},{2,0},{3,1},{4,6},{5,7},{6,4},{7,5},{8,10},{9,11},{10,... | collective-permute-start | bytes 6291464 | tf_op jit(solution)/shard_map/ppermute | solution.py:309
  81.3 91.1 %collective-permute-start.2 = (bf16[256,4096]{1,0:T(8,128)(2,1)}, bf16[256,4096]{1,0:T(8,128)(2,1)}, u32[]{:S(2)}, u32[]{:S(2)}) collective-permute-start(bf16[256,4096]{1,0:T(8,128)(2,1)} %bitcast.3.refs_0_), channel_id=1, source_target_pairs={{0,3},{1,0},{2,1},{3,2},{4,7},{5,4},{6,5},{7,6},{8,11},{9,8},{10,9... | collective-permute-start | bytes 6291464 | tf_op jit(solution)/shard_map/ppermute | solution.py:309
  82.5 270.1 %collective-permute-start.9 = (bf16[1,2,4096,256]{3,2,1,0:T(8,128)(2,1)}, bf16[1,2,4096,256]{3,2,1,0:T(8,128)(2,1)}, u32[]{:S(2)}, u32[]{:S(2)}) collective-permute-start(bf16[1,2,4096,256]{3,2,1,0:T(8,128)(2,1)} %param.22), channel_id=1, source_target_pairs={{0,128},{4,132},{8,136},{12,140},{16,144},{20,148},{24,152},{28,15... | collective-permute-start | bytes 12582920 | tf_op jit(solution)/shard_map/ppermute | solution.py:325
  91.5 92.3 %collective-permute-start.6 = (bf16[256,1024]{1,0:T(8,128)(2,1)}, bf16[256,1024]{1,0:T(8,128)(2,1)S(1)}, u32[]{:S(2)}, u32[]{:S(2)}) collective-permute-start(bf16[256,1024]{1,0:T(8,128)(2,1)} %get-tuple-element.34), channel_id=1, source_target_pairs={{0,1},{1,2},{2,3},{3,0},{4,5},{5,6},{6,7},{7,4},{8,9},{9,10},{10,1... | collective-permute-start | bytes 1572872 | tf_op jit(solution)/shard_map/ppermute | solution.py:309
  125.3 68.5 %collective-permute-start.7 = (bf16[256,1024]{1,0:T(8,128)(2,1)}, bf16[256,1024]{1,0:T(8,128)(2,1)S(1)}, u32[]{:S(2)}, u32[]{:S(2)}) collective-permute-start(bf16[256,1024]{1,0:T(8,128)(2,1)} %get-tuple-element.33), channel_id=1, source_target_pairs={{0,2},{1,3},{2,0},{3,1},{4,6},{5,7},{6,4},{7,5},{8,10},{9,11},{10,... | collective-permute-start | bytes 1572872 | tf_op jit(solution)/shard_map/ppermute | solution.py:309
  171.3 22.5 %copy-start = (bf16[1,256,4096]{2,1,0:T(8,128)(2,1)S(1)}, bf16[1,256,4096]{2,1,0:T(8,128)(2,1)}, u32[]{:S(2)}) copy-start(bf16[1,256,4096]{2,1,0:T(8,128)(2,1)} %param.24) | copy-start | bytes 6291460
  171.3 23.9 %collective-permute-start.8 = (bf16[256,1024]{1,0:T(8,128)(2,1)}, bf16[256,1024]{1,0:T(8,128)(2,1)}, u32[]{:S(2)}, u32[]{:S(2)}) collective-permute-start(bf16[256,1024]{1,0:T(8,128)(2,1)} %get-tuple-element.32), channel_id=1, source_target_pairs={{0,3},{1,0},{2,1},{3,2},{4,7},{5,4},{6,5},{7,6},{8,11},{9,8},{10,9... | collective-permute-start | bytes 1572872 | tf_op jit(solution)/shard_map/ppermute | solution.py:309
  182.9 20.6 %collective-permute-start.3 = (bf16[1024,256]{1,0:T(8,128)(2,1)}, bf16[1024,256]{1,0:T(8,128)(2,1)}, u32[]{:S(2)}, u32[]{:S(2)}) collective-permute-start(bf16[1024,256]{1,0:T(8,128)(2,1)} %gate_up.1.refs_0_), channel_id=1, source_target_pairs={{0,1},{1,2},{2,3},{3,0},{4,5},{5,6},{6,7},{7,4},{8,9},{9,10},{10,1... | collective-permute-start | bytes 1572872 | tf_op jit(solution)/shard_map/ppermute | solution.py:309
  183.8 31.7 %copy-start.4 = (bf16[256,1024]{1,0:T(8,128)(2,1)}, bf16[256,1024]{1,0:T(8,128)(2,1)S(1)}, u32[]{:S(2)}) copy-start(bf16[256,1024]{1,0:T(8,128)(2,1)S(1)} %collective-permute-done.6.refs_5_) | copy-start | bytes 1572868
  183.8 31.7 %collective-permute-start.4 = (bf16[1024,256]{1,0:T(8,128)(2,1)}, bf16[1024,256]{1,0:T(8,128)(2,1)}, u32[]{:S(2)}, u32[]{:S(2)}) collective-permute-start(bf16[1024,256]{1,0:T(8,128)(2,1)} %gate_up.1.refs_0_), channel_id=1, source_target_pairs={{0,2},{1,3},{2,0},{3,1},{4,6},{5,7},{6,4},{7,5},{8,10},{9,11},{10,... | collective-permute-start | bytes 1572872 | tf_op jit(solution)/shard_map/ppermute | solution.py:309
  193.8 21.8 %copy-start.5 = (bf16[256,1024]{1,0:T(8,128)(2,1)}, bf16[256,1024]{1,0:T(8,128)(2,1)S(1)}, u32[]{:S(2)}) copy-start(bf16[256,1024]{1,0:T(8,128)(2,1)S(1)} %collective-permute-done.7.refs_6_) | copy-start | bytes 1572868
  193.8 21.8 %collective-permute-start.5 = (bf16[1024,256]{1,0:T(8,128)(2,1)}, bf16[1024,256]{1,0:T(8,128)(2,1)}, u32[]{:S(2)}, u32[]{:S(2)}) collective-permute-start(bf16[1024,256]{1,0:T(8,128)(2,1)} %gate_up.1.refs_0_), channel_id=1, source_target_pairs={{0,3},{1,0},{2,1},{3,2},{4,7},{5,4},{6,5},{7,6},{8,11},{9,8},{10,9... | collective-permute-start | bytes 1572872 | tf_op jit(solution)/shard_map/ppermute | solution.py:309
  221.9 33.2 %all-to-all-start.2 = ((bf16[8,8,16,1024]{3,2,1,0:T(8,128)(2,1)}), bf16[8,8,16,1024]{3,2,1,0:T(8,128)(2,1)}, u32[]{:S(2)}, u32[]{:S(2)}) async-start(bf16[8,8,16,1024]{3,2,1,0:T(8,128)(2,1)} %bitcast.44), calls=%async_computation.2 | async-start | bytes 4194304 | tf_op jit(solution)/shard_map/all_to_all | solution.py:405
  231.6 120.9 %collective-permute-start.10 = (bf16[216,4096]{1,0:T(8,128)(2,1)}, bf16[216,4096]{1,0:T(8,128)(2,1)}, u32[]{:S(2)}, u32[]{:S(2)}) collective-permute-start(bf16[216,4096]{1,0:T(8,128)(2,1)} %pad_maximum_fusion), channel_id=1, source_target_pairs={{0,128},{4,132},{8,136},{12,140},{16,144},{20,148},{24,152},{28,15... | collective-permute-start | bytes 5308424 | tf_op jit(solution)/shard_map/ppermute | solution.py:325
  232.7 131.9 %collective-permute-start.11 = (bf16[48,4096]{1,0:T(8,128)(2,1)}, bf16[48,4096]{1,0:T(8,128)(2,1)S(1)}, u32[]{:S(2)}, u32[]{:S(2)}) collective-permute-start(bf16[48,4096]{1,0:T(8,128)(2,1)} %slice_bitcast_fusion.5), channel_id=1, source_target_pairs={{0,128},{4,132},{8,136},{12,140},{16,144},{20,148},{24,152},{28,15... | collective-permute-start | bytes 1179656 | tf_op jit(solution)/shard_map/ppermute | solution.py:325
  356.6 28.7 %all-to-all-start.3 = ((bf16[8,64,1024]{2,1,0:T(8,128)(2,1)}), bf16[8,64,1024]{2,1,0:T(8,128)(2,1)S(1)}, u32[]{:S(2)}, u32[]{:S(2)}) async-start(bf16[8,64,1024]{2,1,0:T(8,128)(2,1)} %combine.1), calls=%async_computation.3 | async-start | bytes 2097152 | tf_op jit(solution)/shard_map/all_to_all | solution.py:414
  368.2 23.4 %copy-start.11 = (bf16[1,2,32]{2,1,0:T(2,128)(2,1)S(1)}, bf16[1,2,32]{2,1,0:T(2,128)(2,1)}, u32[]{:S(2)}) copy-start(bf16[1,2,32]{2,1,0:T(2,128)(2,1)} %param.25) | copy-start | bytes 388
  368.2 23.4 %copy-start.12 = (bf16[1,2,32]{2,1,0:T(2,128)(2,1)S(1)}, bf16[1,2,32]{2,1,0:T(2,128)(2,1)}, u32[]{:S(2)}) copy-start(bf16[1,2,32]{2,1,0:T(2,128)(2,1)} %reshape.84) | copy-start | bytes 388
  368.2 23.9 %copy-start.6 = (bf16[1,2,32,2]{3,2,1,0:T(8,128)(2,1)S(1)}, bf16[1,2,32,2]{3,2,1,0:T(8,128)(2,1)}, u32[]{:S(2)}) copy-start(bf16[1,2,32,2]{3,2,1,0:T(8,128)(2,1)} %broadcast_select_fusion.1) | copy-start | bytes 772
  388.2 8.1 %all-to-all-start.4 = ((bf16[4,16,1024]{2,1,0:T(8,128)(2,1)}), bf16[4,16,1024]{2,1,0:T(8,128)(2,1)S(1)}, u32[]{:S(2)}, u32[]{:S(2)}) async-start(bf16[4,16,1024]{2,1,0:T(8,128)(2,1)} %bitcast.48), calls=%async_computation.4 | async-start | bytes 262144 | tf_op jit(solution)/shard_map/all_to_all | solution.py:419
  (7 other events, 43.6 us)

commit v3 on v2

--- a/solution.py
+++ b/solution.py
@@ -304,6 +304,34 @@
     )(parts)
 
 
+def place_rows(flag, fresh, stale, first, count, filled=None):
+    unit = 2 * TOK
+    height, features = stale.shape
+    start = first // unit
+
+    def kernel(f_ref, n_ref, s_ref, *refs):
+        refs[-1][...] = jnp.where(f_ref[0] == 1, n_ref[...], s_ref[...])
+
+    in_specs = [
+        sspec(),
+        pl.BlockSpec((unit, features), lambda i: (i, 0)),
+        pl.BlockSpec((unit, features), lambda i: (start + i, 0)),
+    ]
+    given = [flag, fresh, stale]
+    if filled is not None:
+        in_specs.append(pl.BlockSpec(memory_space=pl.ANY))
+        given.append(filled)
+    return pl.pallas_call(
+        kernel,
+        grid=(count // unit,),
+        in_specs=in_specs,
+        out_specs=pl.BlockSpec((unit, features), lambda i: (start + i, 0)),
+        out_shape=jax.ShapeDtypeStruct((height, features), BF16),
+        input_output_aliases={} if filled is None else {3: 0},
+        name="early_rows" if filled is None else "late_rows",
+    )(*given)
+
+
 def shifted(block, shift):
     copies = lax.axis_size("replica")
     return lax.ppermute(block, "replica", [(i, (i + shift) % copies) for i in range(copies)])
@@ -432,8 +460,10 @@
     gate_up_moved = jnp.where(flagged, gate_up_in, gate_up_values)
     gate_up_scales_moved = jnp.where(flagged, scales_in[0], gate_up_scales)
     down_scales_moved = jnp.where(flagged, scales_in[1], down_scales)
-    down_in = jnp.concatenate([early_in[:cut], late_in])[None]
-    down_moved = jnp.where(flagged, down_in, down_values)
+    flag = flagged.astype(I32).reshape(1)
+    down_moved = place_rows(flag, early_in, down_values[0], 0, cut)
+    late_rows = down_values.shape[1] - cut
+    down_moved = place_rows(flag, late_in, down_values[0], cut, late_rows, down_moved)[None]
     return outputs + (gate_up_moved, gate_up_scales_moved, down_moved, down_scales_moved)
 
 

time: 402 us -> 441 us (1.097)
  waiting for transfers between devices: 236 us -> 275 us
  Pallas kernels: 42.4 us -> 53.4 us
  local copies, waits for them, and re-layouts: 20.4 us -> 13.7 us
  other arithmetic: 14.1 us -> 9.03 us
    all_to_all x1, waiting for transfers between devices: 12.4 us -> 63.6 us  [layer(): lax.all_to_all(mixed, 'expert', 0, 0, tiled=True, axis_index_groups=level...]
    ppermute x3, waiting for transfers between devices: 94 us -> 74.5 us  [swapped(): lax.ppermute(block, 'expert', [(i, (i + half) % experts) for i in range(e...]
    pallas_call x0 -> x2, Pallas kernels: none -> 11 us  [place_rows(): pl.pallas_call(kernel, grid=(count // unit,), in_specs=in_specs, out_spec...]
    all_to_all x1, waiting for transfers between devices: 1 us -> 9.55 us  [layer(): lax.all_to_all(results.reshape(PLANE, levels, -1, width), 'expert', 0, 0,...]
  transfers between devices with their start and end apart: 16 -> 16, of which waited for: 11 -> 11; matrix products, arithmetic and copies ran while one was open for 8% -> 4% of each run, Pallas kernels for 9% -> 11%
where the time goes in v3:
time: 441 us; the launch traced here: 434 us
  waiting for transfers between devices  275 us (62%)
  Pallas kernels  53.4 us (12%)
  blocking collectives  42 us (10%)
  starting transfers between devices  39.8 us (9%)
  local copies, waits for them, and re-layouts  13.7 us (3%)
  other arithmetic  9.03 us (2%)
    ppermute x9, waiting for transfers between devices, shifted(): lax.ppermute(block, 'replica', [(i, (i + shift) % copies) for i in range(...  98.5 us
    ppermute x3, waiting for transfers between devices, swapped(): lax.ppermute(block, 'expert', [(i, (i + half) % experts) for i in range(e...  74.5 us
    all_to_all x1, waiting for transfers between devices, layer(): lax.all_to_all(mixed, 'expert', 0, 0, tiled=True, axis_index_groups=level...  63.6 us
    all_to_all x1, blocking collectives, layer(): lax.all_to_all(own_rows.reshape(PLANE, -1, features), 'expert', 0, 0, til...  31.3 us
    all_to_all x1, waiting for transfers between devices, layer(): lax.all_to_all(packs, 'expert', 0, 0, tiled=True, axis_index_groups=level...  29 us
    ppermute x9, starting transfers between devices, shifted(): lax.ppermute(block, 'replica', [(i, (i + shift) % copies) for i in range(...  11.2 us
    pallas_call x2, Pallas kernels, place_rows(): pl.pallas_call(kernel, grid=(count // unit,), in_specs=in_specs, out_spec...  11 us
    all_gather x1, blocking collectives, layer(): picks = lax.all_gather(column[:, features:], 'replica', axis=0, tiled=True)  10.7 us
  transfers between devices with their start and end apart: 16, of which 11 were waited for; matrix products, arithmetic and copies ran while one was open for 4% of the time, Pallas kernels for 11%

profile of v3, /device:TPU:1, one launch (start us, length us, event | category | flops | bytes accessed | tf_op | source)
XLA Modules:
  0.0 434.4 jit_solution(1524701494985646281)
XLA Ops:
  2.8 9.0 %all-to-all-start = ((bf16[8,16,4224]{2,1,0:T(8,128)(2,1)}), bf16[8,16,4224]{2,1,0:T(8,128)(2,1)S(1)}, u32[]{:S(2)}, u32[]{:S(2)}) async-start(bf16[8,16,4224]{2,1,0:T(8,128)(2,1)} %norm_and_pack.1), calls=%async_computation | async-start | bytes 2162688 | tf_op jit(solution)/shard_map/all_to_all | solution.py:396
  12.7 29.0 %all-to-all-done = bf16[8,16,4224]{2,1,0:T(8,128)(2,1)S(1)} async-done(((bf16[8,16,4224]{2,1,0:T(8,128)(2,1)}), bf16[8,16,4224]{2,1,0:T(8,128)(2,1)S(1)}, u32[]{:S(2)}, u32[]{:S(2)}) %all-to-all-start) | async-done | bytes 1081376 | tf_op jit(solution)/shard_map/all_to_all | solution.py:396
  42.6 3.6 select_rows.1
  46.3 31.3 %all_to_all.25 = bf16[8,32,4096]{2,1,0:T(8,128)(2,1)S(1)} all-to-all(bf16[8,32,4096]{2,1,0:T(8,128)(2,1)} %bitcast.50), channel_id=1, replica_groups={{0,4,8,12,16,20,24,28},{32,36,40,44,48,52,56,60},{64,68,72,76,80,84,88,..., dimensions={0} | all-to-all | bytes 4194304 | tf_op jit(solution)/shard_map/all_to_all | solution.py:411
  83.6 4.6 %down_dequant.1 = bf16[4,256,1024]{2,1,0:T(8,128)(2,1)} custom-call(s32[4]{0:T(128)} %and_select_fusion.order_ref, bf16[256,4096]{1,0:T(8,128)(2,1)} %bitcast.41, f32[2,4096]{1,0:T(2,128)} %bitcast.54), custom_call_target="tpu_custom_call" | custom-call | tf_op jit(solution)/shard_map/down_dequant/pallas_call | solution.py:64
  92.3 32.7 %collective-permute-done.refs_1_ = bf16[256,4096]{1,0:T(8,128)(2,1)} collective-permute-done((bf16[256,4096]{1,0:T(8,128)(2,1)S(1)}, bf16[256,4096]{1,0:T(8,128)(2,1)}, u32[]{:S(2)}, u32[]{:S(2)}) %collective-permute-start) | collective-permute-done | bytes 2097184 | tf_op jit(solution)/shard_map/ppermute | solution.py:337
  126.2 6.8 %gate_up_dequant.1.refs_4_ = bf16[2,4096,256]{2,1,0:T(8,128)(2,1)} custom-call(bf16[2,4096,256]{2,1,0:T(8,128)(2,1)} %bitcast.4.v_ref, f32[2,32,256]{2,1,0:T(8,128)} %reshape.79.s_ref), custom_call_target="tpu_custom_call" | custom-call | tf_op jit(solution)/shard_map/gate_up_dequant/pallas_call | solution.py:41
  133.6 37.4 %collective-permute-done.1.refs_2_ = bf16[256,4096]{1,0:T(8,128)(2,1)} collective-permute-done((bf16[256,4096]{1,0:T(8,128)(2,1)S(1)}, bf16[256,4096]{1,0:T(8,128)(2,1)}, u32[]{:S(2)}, u32[]{:S(2)}) %collective-permute-start.1) | collective-permute-done | bytes 2097184 | tf_op jit(solution)/shard_map/ppermute | solution.py:337
  172.0 10.6 %gate_up.1.refs_0_ = bf16[1024,256]{1,0:T(8,128)(2,1)} custom-call(s32[4]{0:T(128)} %and_select_fusion.1.c_ref, bf16[256,4096]{1,0:T(8,128)(2,1)} %bitcast.47, bf16[256,4096]{1,0:T(8,128)(2,1)} %collective-permute-done.refs_1_, bf16[256,4096]{1,0:T(8,128)(2,1)} %collective-permute-done.1.refs_2_, bf16[256,4096]{1,0:T(8,128)(2,1)} %collective-permute-done.2.refs_3_, ...), custom_call_target="tpu_custom_call" | custom-call | tf_op jit(solution)/shard_map/gate_up/pallas_call | solution.py:162
  183.6 4.2 collective-permute-start.4
  187.7 5.8 %collective-permute-done.7.refs_6_ = bf16[256,1024]{1,0:T(8,128)(2,1)S(1)} collective-permute-done((bf16[256,1024]{1,0:T(8,128)(2,1)}, bf16[256,1024]{1,0:T(8,128)(2,1)S(1)}, u32[]{:S(2)}, u32[]{:S(2)}) %collective-permute-start.7) | collective-permute-done | bytes 524320 | tf_op jit(solution)/shard_map/ppermute | solution.py:337
  193.9 12.0 %collective-permute-done.3.refs_1_ = bf16[1024,256]{1,0:T(8,128)(2,1)S(1)} collective-permute-done((bf16[1024,256]{1,0:T(8,128)(2,1)}, bf16[1024,256]{1,0:T(8,128)(2,1)S(1)}, u32[]{:S(2)}, u32[]{:S(2)}) %collective-permute-start.3) | collective-permute-done | bytes 524320 | tf_op jit(solution)/shard_map/ppermute | solution.py:337
  205.9 8.5 %collective-permute-done.4.refs_2_ = bf16[1024,256]{1,0:T(8,128)(2,1)S(1)} collective-permute-done((bf16[1024,256]{1,0:T(8,128)(2,1)}, bf16[1024,256]{1,0:T(8,128)(2,1)S(1)}, u32[]{:S(2)}, u32[]{:S(2)}) %collective-permute-start.4) | collective-permute-done | bytes 524320 | tf_op jit(solution)/shard_map/ppermute | solution.py:337
  216.3 6.3 %down.1 = bf16[1024,1024]{1,0:T(8,128)(2,1)} custom-call(bf16[1024,256]{1,0:T(8,128)(2,1)} %gate_up.1.refs_0_, bf16[1024,256]{1,0:T(8,128)(2,1)} %copy-done.6, bf16[1024,256]{1,0:T(8,128)(2,1)} %copy-done.7, bf16[1024,256]{1,0:T(8,128)(2,1)} %copy-done.8, bf16[256,1024]{1,0:T(8,128)(2,1)} %get-tuple-element.35.refs_4_, bf16[256,1024]{1,0:T(8,128)(2,1)} %copy-done.4, ...), custom_call_target="tpu_custom_call" | custom-call | tf_op jit(solution)/shard_map/down/pallas_call | solution.py:204
  222.7 6.8 %all-to-all-start.2 = ((bf16[8,8,16,1024]{3,2,1,0:T(8,128)(2,1)}), bf16[8,8,16,1024]{3,2,1,0:T(8,128)(2,1)}, u32[]{:S(2)}, u32[]{:S(2)}) async-start(bf16[8,8,16,1024]{3,2,1,0:T(8,128)(2,1)} %bitcast.48), calls=%async_computation.2 | async-start | bytes 4194304 | tf_op jit(solution)/shard_map/all_to_all | solution.py:433
  232.6 10.7 %all_gather.3.p_ref = bf16[512,128]{1,0:T(8,128)(2,1)} all-gather(bf16[128,128]{1,0:T(8,128)(2,1)S(1)} %slice.53), channel_id=1, replica_groups=mesh['expert'=64,'replica'=4] {'replica'}, dimensions={0}, use_global_device_ids=true | all-gather | bytes 163840 | tf_op jit(solution)/shard_map/all_gather | solution.py:420
  246.3 9.5 %all-to-all-done.2.r_ref = bf16[8,8,16,1024]{3,2,1,0:T(8,128)(2,1)} async-done(((bf16[8,8,16,1024]{3,2,1,0:T(8,128)(2,1)}), bf16[8,8,16,1024]{3,2,1,0:T(8,128)(2,1)}, u32[]{:S(2)}, u32[]{:S(2)}) %all-to-all-start.2) | async-done | bytes 2097184 | tf_op jit(solution)/shard_map/all_to_all | solution.py:433
  255.8 3.3 combine.1
  259.2 3.6 all-to-all-start.3
  262.8 5.4 %collective-permute-start.11 = (bf16[48,4096]{1,0:T(8,128)(2,1)S(1)}, bf16[48,4096]{1,0:T(8,128)(2,1)S(1)}, u32[]{:S(2)}, u32[]{:S(2)}) collective-permute-start(bf16[48,4096]{1,0:T(8,128)(2,1)S(1)} %slice_bitcast_fusion.5), channel_id=1, source_target_pairs={{0,128},{4,132},{8,136},{12,140},{16,144},{20,148},{24,152},{28,15... | collective-permute-start | bytes 1179656 | tf_op jit(solution)/shard_map/ppermute | solution.py:353
  270.1 74.5 %collective-permute-done.10.n_ref = bf16[216,4096]{1,0:T(8,128)(2,1)} collective-permute-done((bf16[216,4096]{1,0:T(8,128)(2,1)}, bf16[216,4096]{1,0:T(8,128)(2,1)}, u32[]{:S(2)}, u32[]{:S(2)}) %collective-permute-start.10) | collective-permute-done | bytes 1769504 | tf_op jit(solution)/shard_map/ppermute | solution.py:353
  346.2 4.6 %broadcast_select_fusion = bf16[1,2,4096,256]{3,2,1,0:T(8,128)(2,1)} fusion(bf16[1,2,4096,256]{3,2,1,0:T(8,128)(2,1)} %collective-permute-done.9, bf16[1,2,4096,256]{3,2,1,0:T(8,128)(2,1)} %param.22, pred[]{:T(512)S(6)} %eq.30), kind=kLoop, calls=%fused_computation | loop fusion | flops 2097152 | bytes 12582913 | tf_op jit(solution)/shard_map/jit(_where)/select_n | solution.py:460
  350.9 63.6 %all-to-all-done.3.p_ref = bf16[8,64,1024]{2,1,0:T(8,128)(2,1)S(1)} async-done(((bf16[8,64,1024]{2,1,0:T(8,128)(2,1)}), bf16[8,64,1024]{2,1,0:T(8,128)(2,1)S(1)}, u32[]{:S(2)}, u32[]{:S(2)}) %all-to-all-start.3) | async-done | bytes 1048608 | tf_op jit(solution)/shard_map/all_to_all | solution.py:442
  421.3 8.3 %early_rows.1.refs_0_ = bf16[256,4096]{1,0:T(8,128)(2,1)} custom-call(s32[1]{0:T(128)} %bitcast.19.f_ref, bf16[216,4096]{1,0:T(8,128)(2,1)} %collective-permute-done.10.n_ref, bf16[256,4096]{1,0:T(8,128)(2,1)} %bitcast.42), custom_call_target="tpu_custom_call" | custom-call | tf_op jit(solution)/shard_map/early_rows/pallas_call | solution.py:324
  (84 shorter events, 40.9 us)
Async XLA Ops:
  0.6 11.1 %copy-start.13 = (s32[64]{0:T(128)S(1)}, s32[64]{0:T(128)}, u32[]{:S(2)}) copy-start(s32[64]{0:T(128)} %param.20) | copy-start | bytes 772
  2.8 38.9 %all-to-all-start = ((bf16[8,16,4224]{2,1,0:T(8,128)(2,1)}), bf16[8,16,4224]{2,1,0:T(8,128)(2,1)S(1)}, u32[]{:S(2)}, u32[]{:S(2)}) async-start(bf16[8,16,4224]{2,1,0:T(8,128)(2,1)} %norm_and_pack.1), calls=%async_computation | async-start | bytes 2162688 | tf_op jit(solution)/shard_map/all_to_all | solution.py:396
  46.3 36.1 %copy-start.11 = (bf16[1,2,32]{2,1,0:T(2,128)(2,1)S(1)}, bf16[1,2,32]{2,1,0:T(2,128)(2,1)}, u32[]{:S(2)}) copy-start(bf16[1,2,32]{2,1,0:T(2,128)(2,1)} %param.25) | copy-start | bytes 388
  77.5 10.6 %copy-start.1 = (bf16[8,32,4096]{2,1,0:T(8,128)(2,1)}, bf16[8,32,4096]{2,1,0:T(8,128)(2,1)S(1)}, u32[]{:S(2)}) copy-start(bf16[8,32,4096]{2,1,0:T(8,128)(2,1)S(1)} %all_to_all.25) | copy-start | bytes 6291460
  77.5 47.5 %collective-permute-start = (bf16[256,4096]{1,0:T(8,128)(2,1)S(1)}, bf16[256,4096]{1,0:T(8,128)(2,1)}, u32[]{:S(2)}, u32[]{:S(2)}) collective-permute-start(bf16[256,4096]{1,0:T(8,128)(2,1)S(1)} %bitcast.44), channel_id=1, source_target_pairs={{0,1},{1,2},{2,3},{3,0},{4,5},{5,6},{6,7},{7,4},{8,9},{9,10},{10,1... | collective-permute-start | bytes 6291464 | tf_op jit(solution)/shard_map/ppermute | solution.py:337
  78.8 92.2 %collective-permute-start.1 = (bf16[256,4096]{1,0:T(8,128)(2,1)S(1)}, bf16[256,4096]{1,0:T(8,128)(2,1)}, u32[]{:S(2)}, u32[]{:S(2)}) collective-permute-start(bf16[256,4096]{1,0:T(8,128)(2,1)S(1)} %bitcast.45), channel_id=1, source_target_pairs={{0,2},{1,3},{2,0},{3,1},{4,6},{5,7},{6,4},{7,5},{8,10},{9,11},{10,... | collective-permute-start | bytes 6291464 | tf_op jit(solution)/shard_map/ppermute | solution.py:337
  81.2 90.7 %collective-permute-start.2 = (bf16[256,4096]{1,0:T(8,128)(2,1)S(1)}, bf16[256,4096]{1,0:T(8,128)(2,1)}, u32[]{:S(2)}, u32[]{:S(2)}) collective-permute-start(bf16[256,4096]{1,0:T(8,128)(2,1)S(1)} %bitcast.46), channel_id=1, source_target_pairs={{0,3},{1,0},{2,1},{3,2},{4,7},{5,4},{6,5},{7,6},{8,11},{9,8},{10,9... | collective-permute-start | bytes 6291464 | tf_op jit(solution)/shard_map/ppermute | solution.py:337
  88.2 37.1 %copy-start.10 = (bf16[1,2,32,2]{2,3,1,0:T(2,128)(2,1)S(1)}, bf16[1,2,32,2]{2,3,1,0:T(2,128)(2,1)}, u32[]{:S(2)}) copy-start(bf16[1,2,32,2]{2,3,1,0:T(2,128)(2,1)} %param.23) | copy-start | bytes 772
  91.1 92.5 %collective-permute-start.6 = (bf16[256,1024]{1,0:T(8,128)(2,1)}, bf16[256,1024]{1,0:T(8,128)(2,1)S(1)}, u32[]{:S(2)}, u32[]{:S(2)}) collective-permute-start(bf16[256,1024]{1,0:T(8,128)(2,1)} %get-tuple-element.34), channel_id=1, source_target_pairs={{0,1},{1,2},{2,3},{3,0},{4,5},{5,6},{6,7},{7,4},{8,9},{9,10},{10,1... | collective-permute-start | bytes 1572872 | tf_op jit(solution)/shard_map/ppermute | solution.py:337
  91.4 102.1 %collective-permute-start.7 = (bf16[256,1024]{1,0:T(8,128)(2,1)}, bf16[256,1024]{1,0:T(8,128)(2,1)S(1)}, u32[]{:S(2)}, u32[]{:S(2)}) collective-permute-start(bf16[256,1024]{1,0:T(8,128)(2,1)} %get-tuple-element.33), channel_id=1, source_target_pairs={{0,2},{1,3},{2,0},{3,1},{4,6},{5,7},{6,4},{7,5},{8,10},{9,11},{10,... | collective-permute-start | bytes 1572872 | tf_op jit(solution)/shard_map/ppermute | solution.py:337
  125.0 219.6 %collective-permute-start.9 = (bf16[1,2,4096,256]{3,2,1,0:T(8,128)(2,1)}, bf16[1,2,4096,256]{3,2,1,0:T(8,128)(2,1)}, u32[]{:S(2)}, u32[]{:S(2)}) collective-permute-start(bf16[1,2,4096,256]{3,2,1,0:T(8,128)(2,1)} %param.22), channel_id=1, source_target_pairs={{0,128},{4,132},{8,136},{12,140},{16,144},{20,148},{24,152},{28,15... | collective-permute-start | bytes 12582920 | tf_op jit(solution)/shard_map/ppermute | solution.py:353
  171.0 22.9 %collective-permute-start.8 = (bf16[256,1024]{1,0:T(8,128)(2,1)}, bf16[256,1024]{1,0:T(8,128)(2,1)}, u32[]{:S(2)}, u32[]{:S(2)}) collective-permute-start(bf16[256,1024]{1,0:T(8,128)(2,1)} %get-tuple-element.32), channel_id=1, source_target_pairs={{0,3},{1,0},{2,1},{3,2},{4,7},{5,4},{6,5},{7,6},{8,11},{9,8},{10,9... | collective-permute-start | bytes 1572872 | tf_op jit(solution)/shard_map/ppermute | solution.py:337
  182.5 23.4 %collective-permute-start.3 = (bf16[1024,256]{1,0:T(8,128)(2,1)}, bf16[1024,256]{1,0:T(8,128)(2,1)S(1)}, u32[]{:S(2)}, u32[]{:S(2)}) collective-permute-start(bf16[1024,256]{1,0:T(8,128)(2,1)} %gate_up.1.refs_0_), channel_id=1, source_target_pairs={{0,1},{1,2},{2,3},{3,0},{4,5},{5,6},{6,7},{7,4},{8,9},{9,10},{10,1... | collective-permute-start | bytes 1572872 | tf_op jit(solution)/shard_map/ppermute | solution.py:337
  183.6 32.0 %copy-start.4 = (bf16[256,1024]{1,0:T(8,128)(2,1)}, bf16[256,1024]{1,0:T(8,128)(2,1)S(1)}, u32[]{:S(2)}) copy-start(bf16[256,1024]{1,0:T(8,128)(2,1)S(1)} %collective-permute-done.6.refs_5_) | copy-start | bytes 1572868
  183.6 30.8 %collective-permute-start.4 = (bf16[1024,256]{1,0:T(8,128)(2,1)}, bf16[1024,256]{1,0:T(8,128)(2,1)S(1)}, u32[]{:S(2)}, u32[]{:S(2)}) collective-permute-start(bf16[1024,256]{1,0:T(8,128)(2,1)} %gate_up.1.refs_0_), channel_id=1, source_target_pairs={{0,2},{1,3},{2,0},{3,1},{4,6},{5,7},{6,4},{7,5},{8,10},{9,11},{10,... | collective-permute-start | bytes 1572872 | tf_op jit(solution)/shard_map/ppermute | solution.py:337
  193.5 22.0 %copy-start.5 = (bf16[256,1024]{1,0:T(8,128)(2,1)}, bf16[256,1024]{1,0:T(8,128)(2,1)S(1)}, u32[]{:S(2)}) copy-start(bf16[256,1024]{1,0:T(8,128)(2,1)S(1)} %collective-permute-done.7.refs_6_) | copy-start | bytes 1572868
  193.5 22.0 %collective-permute-start.5 = (bf16[1024,256]{1,0:T(8,128)(2,1)}, bf16[1024,256]{1,0:T(8,128)(2,1)S(1)}, u32[]{:S(2)}, u32[]{:S(2)}) collective-permute-start(bf16[1024,256]{1,0:T(8,128)(2,1)} %gate_up.1.refs_0_), channel_id=1, source_target_pairs={{0,3},{1,0},{2,1},{3,2},{4,7},{5,4},{6,5},{7,6},{8,11},{9,8},{10,9... | collective-permute-start | bytes 1572872 | tf_op jit(solution)/shard_map/ppermute | solution.py:337
  205.9 9.6 %copy-start.6 = (bf16[1024,256]{1,0:T(8,128)(2,1)}, bf16[1024,256]{1,0:T(8,128)(2,1)S(1)}, u32[]{:S(2)}) copy-start(bf16[1024,256]{1,0:T(8,128)(2,1)S(1)} %collective-permute-done.3.refs_1_) | copy-start | bytes 1572868
  222.7 33.1 %all-to-all-start.2 = ((bf16[8,8,16,1024]{3,2,1,0:T(8,128)(2,1)}), bf16[8,8,16,1024]{3,2,1,0:T(8,128)(2,1)}, u32[]{:S(2)}, u32[]{:S(2)}) async-start(bf16[8,8,16,1024]{3,2,1,0:T(8,128)(2,1)} %bitcast.48), calls=%async_computation.2 | async-start | bytes 4194304 | tf_op jit(solution)/shard_map/all_to_all | solution.py:433
  230.9 113.7 %collective-permute-start.10 = (bf16[216,4096]{1,0:T(8,128)(2,1)}, bf16[216,4096]{1,0:T(8,128)(2,1)}, u32[]{:S(2)}, u32[]{:S(2)}) collective-permute-start(bf16[216,4096]{1,0:T(8,128)(2,1)} %pad_maximum_fusion), channel_id=1, source_target_pairs={{0,128},{4,132},{8,136},{12,140},{16,144},{20,148},{24,152},{28,15... | collective-permute-start | bytes 5308424 | tf_op jit(solution)/shard_map/ppermute | solution.py:353
  259.2 155.3 %all-to-all-start.3 = ((bf16[8,64,1024]{2,1,0:T(8,128)(2,1)}), bf16[8,64,1024]{2,1,0:T(8,128)(2,1)S(1)}, u32[]{:S(2)}, u32[]{:S(2)}) async-start(bf16[8,64,1024]{2,1,0:T(8,128)(2,1)} %combine.1), calls=%async_computation.3 | async-start | bytes 2097152 | tf_op jit(solution)/shard_map/all_to_all | solution.py:442
  262.8 167.5 %collective-permute-start.11 = (bf16[48,4096]{1,0:T(8,128)(2,1)S(1)}, bf16[48,4096]{1,0:T(8,128)(2,1)S(1)}, u32[]{:S(2)}, u32[]{:S(2)}) collective-permute-start(bf16[48,4096]{1,0:T(8,128)(2,1)S(1)} %slice_bitcast_fusion.5), channel_id=1, source_target_pairs={{0,128},{4,132},{8,136},{12,140},{16,144},{20,148},{24,152},{28,15... | collective-permute-start | bytes 1179656 | tf_op jit(solution)/shard_map/ppermute | solution.py:353
  346.2 74.6 %copy-start.12 = (bf16[1,2,32]{2,1,0:T(2,128)(2,1)S(1)}, bf16[1,2,32]{2,1,0:T(2,128)(2,1)}, u32[]{:S(2)}) copy-start(bf16[1,2,32]{2,1,0:T(2,128)(2,1)} %param.25) | copy-start | bytes 388
  417.4 16.3 %all-to-all-start.4 = ((bf16[4,16,1024]{2,1,0:T(8,128)(2,1)}), bf16[4,16,1024]{2,1,0:T(8,128)(2,1)S(1)}, u32[]{:S(2)}, u32[]{:S(2)}) async-start(bf16[4,16,1024]{2,1,0:T(8,128)(2,1)} %bitcast.53), calls=%async_computation.4 | async-start | bytes 262144 | tf_op jit(solution)/shard_map/all_to_all | solution.py:447
  (6 other events, 11.4 us)
